TPU v7x, 32 devices: a whole 2x2x4 slice. The times are simulated.
32 devices in a mesh: section: 4 (over z), dp: 8 (over y, x, core).
Axes of the slice: x: 2, y: 2, z: 4, core: 2. Of those that a mesh axis runs over, the one named last changes fastest.
Arguments:
- activations: bfloat16 [4, 4, 2048, 1280], P('section', None, 'dp'), may hold values from -6 to 6
- cotangent: bfloat16 [4, 2048, 1280], P(None, 'dp'), may hold values from -1.5 to 1.5
- counts: int32 [4, 8], P(None, 'dp'), may hold values from 64 to 256
- arrival: int32 [4], replicated, may hold values from 0 to 3, each once
- norm_gain: float32 [4, 1280], P('section'), may hold values from 0.1 to 1.9
- qkv_weight: bfloat16 [4, 1280, 1920], P('section'), may hold values from -8 to 8
- out_weight: bfloat16 [4, 1280, 640], P('section'), may hold values from -0.25 to 0.25
Outputs:
- qkv_grad: float32 [4, 1280, 1920], P('section', 'dp')
- out_grad: float32 [4, 1280, 640], P('section', 'dp')
Inputs may be any that keep to these rules, and one draw needn't show every extreme that they name: `arrival`: each microbatch once.
All inputs are finite; a program needn't handle non-finite values.
Results may differ from a plain program's by a relative error of at most 0.025.
Values may be sent and summed in bfloat16 or wider, within the bound.
No kernel may reach another device: no remote copies, remote signals or barrier semaphores. Data moves between devices by JAX's collectives and lax.ppermute only.
A program may use at most 128 MiB of HBM per device.

v0:
```python
import functools

import jax
import jax.numpy as jnp
from jax import lax
from jax.experimental import pallas as pl
from jax.experimental.pallas import tpu as pltpu
from jax.sharding import PartitionSpec as P

HDIM = 80
HEADS = 8
EPSILON = 1e-06
SCALE = HDIM ** (-0.5)
LOG2_E = 1.4426950408889634
HALF = HEADS // 2
ROWS_AT_A_TIME = 128
WIDTH_CHUNKS = 5

BF = jnp.bfloat16
F32 = jnp.float32
VMEM = pl.BlockSpec(memory_space=pltpu.VMEM)
SMEM = pl.BlockSpec(memory_space=pltpu.SMEM)
ANY = pl.BlockSpec(memory_space=pl.ANY)
HBM = pl.BlockSpec(memory_space=pltpu.HBM)
SCRATCH = {
    "recompute_first": 8192,
    "recompute": 6144,
    "backward": 5120,
    "weights": 3072,
    "tail_out": 3072,
    "tail_qkv": 3072,
    "halve_out": 3072,
    "halve": 3072,
    "finish": 3072,
}

RECOMPUTED = ("packed", "values", "probs", "normed", "hidden", "attn", "inv_std", "masked", "inputs")
COTANGENTS = ("grad_packed", "masked")


def contract(left, right, dims=(1, 0)):
    return lax.dot_general(left, right, ((dims[:1], dims[1:]), ((), ())), preferred_element_type=F32)


def head_rows(part, h):
    return pl.ds(pl.multiple_of(part * (HEADS * HDIM) + h * HDIM, 16), HDIM)


def staged(heads, first, second, third):
    first(0, 0)
    first(1, 1)
    second(0, 0)

    def two_steps(i, _):
        h = 2 * i
        third(h, 0)
        second(h + 1, 1)
        first(h + 2, 0)
        third(h + 1, 1)
        second(h + 2, 0)
        first(h + 3, 1)
        return 0

    lax.fori_loop(0, (heads - 2) // 2, two_steps, 0)
    second(heads - 1, 1)
    third(heads - 2, 0)
    third(heads - 1, 1)


def over_lanes(column, lanes):
    return jnp.concatenate([column] * (lanes // column.shape[1]), axis=1)


def normalize(position, x_buf, gain, normed, hidden, inv_std, rows_hidden, unit_rows, inv_rows):
    slots = x_buf.shape[0]

    def some_rows(i, _):
        rows = pl.ds(pl.multiple_of(i * ROWS_AT_A_TIME, ROWS_AT_A_TIME), ROWS_AT_A_TIME)
        floats = x_buf[rows, :].astype(F32)
        centered = floats - jnp.mean(floats, axis=-1, keepdims=True)
        inv = lax.rsqrt(jnp.mean(centered * centered, axis=-1, keepdims=True) + EPSILON)
        unit = centered * inv
        unit_rows[rows, :] = unit.astype(BF)
        inv_rows[rows, :] = jnp.broadcast_to(inv, (ROWS_AT_A_TIME, inv_rows.shape[1]))
        rows_hidden[rows, :] = (unit * gain[0:1, :]).astype(BF)
        return 0

    lax.fori_loop(0, slots // ROWS_AT_A_TIME, some_rows, 0)
    inv_std[position] = inv_rows[...].T[0:8, :]


def project(position, part, w_qkv, packed, values, queries, keys, rows_hidden):
    width = HEADS * HDIM
    got = contract(rows_hidden[...], w_qkv[:, part * width : (part + 1) * width]).astype(BF)
    turned = got.T
    packed[position, part * width : (part + 1) * width, :] = turned
    for h in range(HEADS):
        cols = slice(h * HDIM, (h + 1) * HDIM)
        if part == 0:
            queries[h, 0:HDIM, :] = turned[cols, :]
        if part == 1:
            keys[h, :, 0:HDIM] = got[:, cols]
        if part == 2:
            values[position * HEADS + h] = got[:, cols]


def exclude_keys(count, queries, keys):
    extra = queries.shape[1] - HDIM
    slots = keys.shape[1]
    ones = lax.broadcasted_iota(jnp.int32, (extra, slots), 0) == 0
    ones = jnp.where(ones, 1.0, 0.0).astype(BF)
    past = (lax.broadcasted_iota(jnp.int32, (slots, extra), 0) >= count) & (
        lax.broadcasted_iota(jnp.int32, (slots, extra), 1) == 0
    )
    low = jnp.where(past, -1e30, 0.0).astype(BF)
    for h in range(HEADS):
        queries[h, HDIM:, :] = ones
        keys[h, :, HDIM:] = low


def attend(position, packed, probs, attn, queries, keys, scores, halves):
    def score(h, slot):
        scores[slot][...] = contract(keys[h], queries[h])

    def soften(h, slot):
        raw = scores[slot][...]
        raised = jnp.exp2((raw - jnp.max(raw, axis=0, keepdims=True)) * (SCALE * LOG2_E))
        prob = (raised * (1.0 / jnp.sum(raised, axis=0, keepdims=True))).astype(BF)
        probs[position * HEADS + h] = prob
        halves[slot][...] = prob

    def mix(h, slot):
        attn[position, head_rows(0, h), :] = contract(packed[position, head_rows(2, h), :], halves[slot][...]).astype(BF)

    staged(HEADS, score, soften, mix)


def recompute_body(position, sections, scalars, x_hbm, own, gain, w_qkv, *refs, before_part=None):
    packed, values, probs, normed, hidden, attn, inv_std, masked, inputs = refs[-22:-13]
    rows_hidden, unit_rows, inv_rows, queries, keys, g_buf = refs[-13:-7]
    scores, halves, sems = refs[-7:-5], refs[-5:-3], refs[-3:]
    micro_count = packed.shape[0]
    micro = scalars[2 + position]
    count = scalars[2 + micro_count + micro]
    is_last = scalars[0] == sections - 1
    own_copy = pltpu.make_async_copy(own.at[position], g_buf, sems[1])
    x_buf = inputs.at[position % 2]
    if position == 0:
        copy = pltpu.make_async_copy(x_hbm.at[0, micro], x_buf, sems[0])
        copy.start()
        for part in before_part:
            part.start()
        copy.wait()
    if position + 1 < micro_count:
        following = pltpu.make_async_copy(
            x_hbm.at[0, scalars[3 + position]], inputs.at[(position + 1) % 2], sems[2]
        )
        following.start()

    @pl.when(is_last)
    def _():
        own_copy.start()

    exclude_keys(count, queries, keys)
    normalize(position, x_buf, gain, normed, hidden, inv_std, rows_hidden, unit_rows, inv_rows)
    for part in range(3):
        if before_part is not None:
            before_part[part].wait()
        project(position, part, w_qkv, packed, values, queries, keys, rows_hidden)
        if part == 0:
            normed[position] = unit_rows[...].T
        if part == 1:
            hidden[position] = rows_hidden[...].T
    attend(position, packed, probs, attn, queries, keys, scores, halves)

    @pl.when(is_last)
    def _():
        own_copy.wait()
        turned = g_buf[...].T
        ids = lax.broadcasted_iota(jnp.int32, turned.shape, 1)
        masked[position] = jnp.where(ids < count, turned.astype(F32), 0.0).astype(BF)

    if position + 1 < micro_count:
        following.wait()


def first_body(sections, scalars, x_hbm, own, gain, wq_hbm, wo_hbm, *refs):
    wq, wo_t, gain_t = refs[:3]
    wo, part_sems = refs[-2:]
    width = HEADS * HDIM
    parts = []
    for part in range(3):
        cols = pl.ds(part * width, width)
        parts.append(pltpu.make_async_copy(wq_hbm.at[0, :, cols], wq.at[:, cols], part_sems.at[part]))
    parts.append(pltpu.make_async_copy(wo_hbm.at[0], wo, part_sems.at[3]))
    recompute_body(0, sections, scalars, x_hbm, own, gain, wq, *refs[3:-2], before_part=parts)
    gain_t[...] = jnp.broadcast_to(gain[0:1, :], (gain_t.shape[1], gain.shape[1])).T
    parts[3].wait()
    wo_t[...] = wo[...].T


def heads_backward(position, start, heads, gattn, packed, values, probs, out, offsets, grads, halves):
    def g_rows(h):
        return gattn[pl.ds(pl.multiple_of((start + h) * HDIM, 16), HDIM), :]

    def keep(part, h, value):
        rows = pl.ds(pl.multiple_of(offsets[part] + h * HDIM, 16), HDIM)
        out[rows, :] = value.astype(BF)

    def through_values(h, slot):
        grads[slot][...] = contract(values[position * HEADS + start + h], g_rows(h))

    def through_softmax(h, slot):
        grad_prob = grads[slot][...]
        full = probs[position * HEADS + start + h].astype(F32)
        inner = jnp.sum(full * grad_prob, axis=0, keepdims=True)
        halves[slot][...] = (full * (grad_prob - inner)).astype(BF)

    def through_scores(h, slot):
        grad_s = halves[slot][...]
        keep(0, h, contract(packed[position, head_rows(1, start + h), :], grad_s) * SCALE)
        keep(1, h, contract(packed[position, head_rows(0, start + h), :], grad_s, (1, 1)) * SCALE)
        keep(2, h, contract(g_rows(h), probs[position * HEADS + start + h], (1, 1)))

    staged(heads, through_values, through_softmax, through_scores)


def placing(slot, sections, scalars, micro_count):
    section = scalars[0]
    position = slot - 2 * (sections - 1 - section)
    valid = (position >= 0) & (position < micro_count)
    position = jnp.clip(position, 0, micro_count - 1)
    count = scalars[2 + micro_count + scalars[2 + position]]
    return section, position, valid, count


def take_arriving(sections, section, arriving, position, masked):
    if arriving is not None:

        @pl.when(section != sections - 1)
        def _():
            masked[position] = arriving[...]


def backward_body(slot, sections, has_arriving, passes, scalars, *refs):
    arriving = None
    if has_arriving:
        arriving, refs = refs[0], refs[1:]
    wq, wo_t, gain_t, packed, values, probs, normed, inv_std = refs[:8]
    if passes:
        passed, refs = refs[-9], (*refs[:-9], *refs[-8:])
    grad_packed, masked, gattn, grad_hidden = refs[-8:-4]
    grads, halves = refs[-4:-2], refs[-2:]
    section, position, valid, count = placing(slot, sections, scalars, masked.shape[0])
    width, slots = masked.shape[1:]

    @pl.when(valid)
    def _():
        take_arriving(sections, section, arriving, position, masked)
        gattn[...] = contract(wo_t[...], masked[position]).astype(BF)
        span = HEADS * HDIM
        heads_backward(
            position,
            0,
            HEADS,
            gattn,
            packed,
            values,
            probs,
            grad_packed.at[position],
            (0, span, 2 * span),
            grads,
            halves,
        )

    if not passes:
        return

    @pl.when(valid & (section > 0))
    def _():
        chunk = width // WIDTH_CHUNKS

        def some_width(i, carry):
            total, along = carry
            rows = pl.ds(pl.multiple_of(i * chunk, 16), chunk)
            got = contract(wq[rows, :], grad_packed[position]) * over_lanes(gain_t[rows, :], slots)
            grad_hidden[rows, :] = got
            unit = normed[position, rows, :].astype(F32)
            total = total + jnp.sum(got, axis=0, keepdims=True)
            along = along + jnp.sum(got * unit, axis=0, keepdims=True)
            return total, along

        zero = jnp.zeros((1, slots), F32)
        total, along = lax.fori_loop(0, WIDTH_CHUNKS, some_width, (zero, zero))
        mean = total * (1.0 / width)
        along = along * (1.0 / width)
        shown = lax.broadcasted_iota(jnp.int32, (1, slots), 1) < count
        inv = jnp.where(shown, inv_std[position, 0:1, :], 0.0)

        def finish(i, _):
            rows = pl.ds(pl.multiple_of(i * chunk, 16), chunk)
            unit = normed[position, rows, :].astype(F32)
            grad_ln = inv * (grad_hidden[rows, :] - mean - unit * along)
            passed[rows, :] = (masked[position, rows, :].astype(F32) + grad_ln).astype(BF)
            return 0

        lax.fori_loop(0, WIDTH_CHUNKS, finish, 0)


def gather_half(source, half, compact):
    width = HEADS * HDIM
    span = HALF * HDIM
    for part in range(3):
        at = part * width + half * span
        compact[part * span : (part + 1) * span, :] = source[at : at + span, :]


def weights_body(index, hidden, attn, grad_packed, masked, *refs):
    acc_out, compact = refs[-2:]
    acc_qkv = refs[-4:-2]
    width = hidden.shape[1]
    chunk = width // 5

    def some_width(i, _):
        rows = pl.ds(pl.multiple_of(i * chunk, 16), chunk)
        for half in range(2):
            total = contract(hidden[index, rows, :], compact[half], (1, 1))
            if index > 0:
                total = total + acc_qkv[half][rows, :].astype(F32)
            acc_qkv[half][rows, :] = total.astype(BF)
        total = contract(masked[index, rows, :], attn[index], (1, 1))
        if index > 0:
            total = total + acc_out[rows, :].astype(F32)
        acc_out[rows, :] = total.astype(BF)
        return 0

    for half in range(2):
        gather_half(grad_packed.at[index], half, compact.at[half])
    lax.fori_loop(0, 5, some_width, 0)


def blocks_out(dp_index, left, right, acc, sent, kept):
    count, block = sent.shape[:2]

    def one(j, target, to):
        at = pl.multiple_of((dp_index ^ j) * block, 16)
        value = contract(left[pl.ds(at, block), :], right, (1, 1)) + acc[pl.ds(at, block), :].astype(F32)
        target[to] = value.astype(BF)

    def two(i, _):
        one(2 * i + 1, sent, i)
        one(2 * i, kept, i)
        return 0

    lax.fori_loop(0, count, two, 0)


def tail_out_body(slot, sections, has_arriving, scalars, *refs):
    arriving = None
    if has_arriving:
        arriving, refs = refs[0], refs[1:]
    attn, acc_out = refs[:2]
    sent, kept, masked = refs[-3:]
    section, position, valid, _ = placing(slot, sections, scalars, masked.shape[0])
    last = masked.shape[0] - 1

    @pl.when(valid)
    def _():
        take_arriving(sections, section, arriving, position, masked)

    blocks_out(scalars[1], masked.at[last], attn[last], acc_out, sent, kept)


def tail_half_body(slot, sections, half, scalars, wo_t, packed, values, probs, masked, hidden, acc_qkv, gp_all, *refs):
    sent, kept, gattn, compact = refs[-8:-4]
    grads, halves = refs[-4:-2], refs[-2:]
    _, position, valid, _ = placing(slot, sections, scalars, masked.shape[0])
    last = masked.shape[0] - 1
    span = HALF * HDIM

    @pl.when(valid)
    def _():
        rows = slice(half * span, (half + 1) * span)
        gattn[rows, :] = contract(wo_t[rows, :], masked[position]).astype(BF)
        heads_backward(
            position,
            half * HALF,
            HALF,
            gattn,
            packed,
            values,
            probs,
            compact,
            (0, span, 2 * span),
            grads,
            halves,
        )

    @pl.when(jnp.logical_not(valid))
    def _():
        gather_half(gp_all.at[last], half, compact)

    blocks_out(scalars[1], hidden.at[last], compact[...], acc_qkv, sent, kept)


def halve_out_body(split, keeps, sends, kept, arrived, *outs):
    for piece, cols in enumerate((slice(0, split), slice(split, kept.shape[2]))):
        kept_out, sent_out = outs[2 * piece : 2 * piece + 2]
        for target, sources in ((kept_out, keeps[piece]), (sent_out, sends[piece])):
            for j, source in enumerate(sources):
                target[j] = (kept[source, :, cols].astype(F32) + arrived[source, :, cols].astype(F32)).astype(BF)


def halve_body(keeps, sends, kept, arrived, kept_out, sent_out):
    for j, source in enumerate(keeps):
        kept_out[j] = (kept[source].astype(F32) + arrived[source].astype(F32)).astype(BF)
    for j, source in enumerate(sends):
        sent_out[j] = (kept[source].astype(F32) + arrived[source].astype(F32)).astype(BF)


def finish_body(split, *refs):
    qkv, out = refs[-2:]
    span = HALF * HDIM
    width = HEADS * HDIM
    for half in range(2):
        kept, arrived = refs[2 * half : 2 * half + 2]
        total = kept[0].astype(F32) + arrived[0].astype(F32)
        for part in range(3):
            at = part * width + half * span
            qkv[:, at : at + span] = total[:, part * span : (part + 1) * span]
    for piece, cols in enumerate((slice(0, split), slice(split, out.shape[1]))):
        kept, arrived = refs[4 + 2 * piece : 6 + 2 * piece]
        out[:, cols] = kept[0].astype(F32) + arrived[0].astype(F32)


def kept_on_chip(shape, dtype):
    return pltpu.VMEM(shape, dtype)


def per_device(activations, cotangent, counts, arrival, norm_gain, qkv_weight, out_weight):
    sections = lax.axis_size("section")
    dp_count = lax.axis_size("dp")
    section = lax.axis_index("section")
    dp_index = lax.axis_index("dp")
    micro_count, slots, width = cotangent.shape
    packed_width = qkv_weight.shape[2]
    head_width = out_weight.shape[2]
    span = packed_width // 2
    block = width // dp_count
    activations, cotangent, qkv_weight, out_weight = (
        pltpu.with_memory_space_constraint(x, pltpu.HBM)
        for x in (activations, cotangent, qkv_weight, out_weight)
    )
    scalars = jnp.concatenate([jnp.stack([section, dp_index]).astype(jnp.int32), arrival, counts[:, 0]])

    shapes = {
        "packed": kept_on_chip((micro_count, packed_width, slots), BF),
        "values": kept_on_chip((micro_count * HEADS, slots, HDIM), BF),
        "probs": kept_on_chip((micro_count * HEADS, slots, slots), BF),
        "normed": kept_on_chip((micro_count, width, slots), BF),
        "hidden": kept_on_chip((micro_count, width, slots), BF),
        "attn": kept_on_chip((micro_count, head_width, slots), BF),
        "inv_std": kept_on_chip((micro_count, 8, slots), F32),
        "grad_packed": kept_on_chip((micro_count, packed_width, slots), BF),
        "inputs": kept_on_chip((2, slots, width), BF),
        "masked": kept_on_chip((micro_count, width, slots), BF),
    }
    head_scratch = [pltpu.VMEM((slots, slots), F32)] * 2 + [pltpu.VMEM((slots, slots), BF)] * 2
    row_scratch = [
        pltpu.VMEM((slots, width), BF),
        pltpu.VMEM((slots, width), BF),
        pltpu.VMEM((slots, 128), F32),
        pltpu.VMEM((HEADS, HDIM + 16, slots), BF),
        pltpu.VMEM((HEADS, slots, HDIM + 16), BF),
        pltpu.VMEM((slots, width), BF),
        *head_scratch,
        pltpu.SemaphoreType.DMA,
        pltpu.SemaphoreType.DMA,
        pltpu.SemaphoreType.DMA,
    ]
    state = {}

    def recompute(position, weights):
        outs = tuple(shapes[name] for name in RECOMPUTED)
        if position == 0:
            results = pl.pallas_call(
                functools.partial(first_body, sections),
                out_shape=(
                    kept_on_chip(qkv_weight.shape[1:], BF),
                    kept_on_chip((head_width, width), BF),
                    kept_on_chip((width, 128), F32),
                    *outs,
                ),
                in_specs=[SMEM, HBM, HBM, VMEM, HBM, HBM],
                out_specs=(VMEM,) * (3 + len(outs)),
                scratch_shapes=row_scratch + [pltpu.VMEM((width, head_width), BF), pltpu.SemaphoreType.DMA((4,))],
                compiler_params=pltpu.CompilerParams(vmem_limit_bytes=SCRATCH["recompute_first"] << 10),
                name="recompute_first",
            )(scalars, activations, cotangent, norm_gain, qkv_weight, out_weight)
            state.update(zip(RECOMPUTED, results[3:]))
            return results[:3]
        results = pl.pallas_call(
            functools.partial(recompute_body, position, sections),
            out_shape=outs,
            in_specs=[SMEM, HBM, HBM, VMEM, VMEM] + [ANY] * len(outs),
            out_specs=(VMEM,) * len(outs),
            scratch_shapes=row_scratch,
            input_output_aliases={5 + i: i for i in range(len(outs))},
            compiler_params=pltpu.CompilerParams(vmem_limit_bytes=SCRATCH["recompute"] << 10),
            name="recompute",
        )(scalars, activations, cotangent, norm_gain, weights[0], *(state[name] for name in RECOMPUTED))
        state.update(zip(RECOMPUTED, results))
        return weights

    def backward(slot, arriving, weights, passes):
        extra = [] if arriving is None else [arriving]
        outs = tuple(shapes[name] for name in COTANGENTS)
        if passes:
            outs = (jax.ShapeDtypeStruct((width, slots), BF), *outs)
        operands = [scalars, *extra, *weights]
        operands += [state[name] for name in ("packed", "values", "probs", "normed", "inv_std")]
        specs = [SMEM] + [VMEM] * (len(operands) - 1)
        given = [name for name in COTANGENTS if name in state]
        aliases = {len(operands) + i: passes + COTANGENTS.index(name) for i, name in enumerate(given)}
        operands += [state[name] for name in given]
        specs += [ANY] * len(given)
        results = pl.pallas_call(
            functools.partial(backward_body, slot, sections, arriving is not None, passes),
            out_shape=outs,
            in_specs=specs,
            out_specs=(VMEM,) * len(outs),
            scratch_shapes=[
                pltpu.VMEM((head_width, slots), BF),
                pltpu.VMEM((width, slots), F32),
                *head_scratch,
            ],
            input_output_aliases=aliases,
            compiler_params=pltpu.CompilerParams(vmem_limit_bytes=SCRATCH["backward"] << 10),
            name="backward",
        )(*operands)
        state.update(zip(COTANGENTS, results[-2:]))
        return results[0]

    def weights_step(index):
        operands = [state[name] for name in ("hidden", "attn", "grad_packed", "masked")]
        specs = [VMEM] * len(operands)
        aliases = {}
        if index > 0:
            aliases = {len(operands) + i: i for i in range(3)}
            operands += state["sums"]
            specs += [ANY] * 3
        state["sums"] = pl.pallas_call(
            functools.partial(weights_body, index),
            out_shape=(
                kept_on_chip((width, span), BF),
                kept_on_chip((width, span), BF),
                kept_on_chip((width, head_width), BF),
            ),
            in_specs=specs,
            out_specs=(VMEM,) * 3,
            scratch_shapes=[pltpu.VMEM((2, span, slots), BF)],
            input_output_aliases=aliases,
            compiler_params=pltpu.CompilerParams(vmem_limit_bytes=SCRATCH["weights"] << 10),
            name="weights",
        )(*operands)

    def exchange(value, bit):
        pairs = [(source, source ^ bit) for source in range(dp_count)]
        return lax.ppermute(value, "dp", pairs)

    def halve(kept, arrived, bit, held):
        keeps = [i for i, j in enumerate(held) if not j & bit]
        sends = [i for i, j in enumerate(held) if j & bit]
        shape = (len(keeps), *kept.shape[1:])
        kept, sent = pl.pallas_call(
            functools.partial(halve_body, keeps, sends),
            out_shape=(jax.ShapeDtypeStruct(shape, BF), jax.ShapeDtypeStruct(shape, BF)),
            in_specs=[VMEM, VMEM],
            out_specs=(VMEM, VMEM),
            compiler_params=pltpu.CompilerParams(vmem_limit_bytes=SCRATCH["halve"] << 10),
            name="halve",
        )(kept, arrived)
        return kept, exchange(sent, bit), [held[i] for i in keeps]

    last_slot = micro_count + 2 * (sections - 1) - 1
    in_flight = {}
    weights = None
    for slot in range(last_slot):
        if slot < micro_count:
            weights = recompute(slot, weights)
        pairs = [
            (s, s - 1)
            for s in range(1, sections)
            if 0 <= slot - 2 * (sections - 1 - s) < micro_count
        ]
        passed = backward(slot, in_flight.pop(slot, None), weights, bool(pairs))
        if pairs:
            in_flight[slot + 2] = lax.ppermute(passed, "section", pairs)
        index = slot - 2 * (sections - 1)
        if 0 <= index < micro_count - 1:
            weights_step(index)

    arriving = in_flight.pop(last_slot, None)
    extra = [] if arriving is None else [arriving]
    pair_shape = (dp_count // 2, block)
    operands = [scalars, *extra, state["attn"], state["sums"][2], state["masked"]]
    sent_out, kept_out, masked = pl.pallas_call(
        functools.partial(tail_out_body, last_slot, sections, arriving is not None),
        out_shape=(
            jax.ShapeDtypeStruct((*pair_shape, head_width), BF),
            jax.ShapeDtypeStruct((*pair_shape, head_width), BF),
            shapes["masked"],
        ),
        in_specs=[SMEM] + [VMEM] * (len(operands) - 2) + [ANY],
        out_specs=(VMEM,) * 3,
        input_output_aliases={len(operands) - 1: 2},
        compiler_params=pltpu.CompilerParams(vmem_limit_bytes=SCRATCH["tail_out"] << 10),
        name="tail_out",
    )(*operands)
    arrived_out = exchange(sent_out, 1)

    def tail_half(half, scalars):
        sent, kept = pl.pallas_call(
            functools.partial(tail_half_body, last_slot, sections, half),
            out_shape=(
                jax.ShapeDtypeStruct((*pair_shape, span), BF),
                jax.ShapeDtypeStruct((*pair_shape, span), BF),
            ),
            in_specs=[SMEM] + [VMEM] * 8,
            out_specs=(VMEM, VMEM),
            scratch_shapes=[pltpu.VMEM((head_width, slots), BF), pltpu.VMEM((span, slots), BF), *head_scratch],
            compiler_params=pltpu.CompilerParams(vmem_limit_bytes=SCRATCH["tail_qkv"] << 10),
            name="tail_qkv",
        )(
            scalars,
            weights[1],
            state["packed"],
            state["values"],
            state["probs"],
            masked,
            state["hidden"],
            state["sums"][half],
            state["grad_packed"],
        )
        return kept, exchange(sent, 1)

    bits = [1 << i for i in range(1, dp_count.bit_length() - 1)]
    held = list(range(0, dp_count, 2))
    split = head_width // 256 * 128
    first = tail_half(0, scalars)
    keeps = [[i for i, j in enumerate(held) if not j & bit] for bit in (bits[0], bits[-1])]
    sends = [[i for i, j in enumerate(held) if j & bit] for bit in (bits[0], bits[-1])]
    piece_shapes = [
        jax.ShapeDtypeStruct((len(held) // 2, block, cols), BF)
        for cols in (split, split, head_width - split, head_width - split)
    ]
    kept_a, sent_a, kept_b, sent_b = pl.pallas_call(
        functools.partial(halve_out_body, split, keeps, sends),
        out_shape=tuple(piece_shapes),
        in_specs=[VMEM, VMEM],
        out_specs=(VMEM,) * 4,
        compiler_params=pltpu.CompilerParams(vmem_limit_bytes=SCRATCH["halve_out"] << 10),
        name="halve_out",
    )(kept_out, arrived_out)
    later_scalars, kept_a, sent_a, kept_b, sent_b = lax.optimization_barrier(
        (scalars, kept_a, sent_a, kept_b, sent_b)
    )
    out_streams = [
        (kept_a, exchange(sent_a, bits[0]), [held[i] for i in keeps[0]]),
        (kept_b, exchange(sent_b, bits[-1]), [held[i] for i in keeps[1]]),
    ]
    second = tail_half(1, later_scalars)
    orders = [bits, bits[::-1]]
    qkv_streams = [(*first, held), (*second, held)]
    for step in range(len(bits)):
        if step > 0:
            for i in range(2):
                out_streams[i] = halve(*out_streams[i][:2], orders[i][step], out_streams[i][2])
        for i in range(2):
            qkv_streams[i] = halve(*qkv_streams[i][:2], orders[i][step], qkv_streams[i][2])
    flat = [x for kept, arrived, _ in qkv_streams + out_streams for x in (kept, arrived)]
    qkv_share, out_share = pl.pallas_call(
        functools.partial(finish_body, split),
        out_shape=(
            jax.ShapeDtypeStruct((block, packed_width), F32),
            jax.ShapeDtypeStruct((block, head_width), F32),
        ),
        in_specs=[VMEM] * len(flat),
        out_specs=(VMEM, VMEM),
        compiler_params=pltpu.CompilerParams(vmem_limit_bytes=SCRATCH["finish"] << 10),
        name="finish",
    )(*flat)
    return (qkv_share[None], out_share[None])


def solution(mesh):
    placed = (
        P("section", None, "dp", None),
        P(None, "dp", None),
        P(None, "dp"),
        P(),
        P("section", None),
        P("section", None, None),
        P("section", None, None),
    )
    return jax.shard_map(
        per_device,
        mesh=mesh,
        in_specs=placed,
        out_specs=(P("section", "dp", None), P("section", "dp", None)),
        check_vma=False,
    )
```

profile of v0, /device:TPU:0, one launch (start us, length us, event | category | flops | bytes accessed | tf_op | source)
XLA Modules:
  0.0 174.7 jit_solution(12098335427328157137)
XLA Ops:
  2.1 9.0 %recompute_first.1 = (bf16[1280,1920]{1,0:T(8,128)(2,1)S(1)}, bf16[640,1280]{1,0:T(8,128)(2,1)S(1)}, f32[1280,128]{1,0:T(8,128)S(1)}, bf16[4,1920,256]{2,1,0:T(8...) custom-call(s32[10]{0:T(128)S(1)} %pad_add_fusion.scalars, ...), custom_call_target="tpu_custom_call" | custom-call | tf_op jit(solution)/shard_map/recompute_first/pallas_call | solution.py:486
  12.4 4.5 %recompute.3 = (bf16[4,1920,256]{2,1,0:T(8,128)(2,1)S(1)}, bf16[32,256,80]{2,1,0:T(8,128)(2,1)S(1)}, bf16[32,256,256]{2,1,0:T(8,128)(2,1)S(1)}, bf16[4,1280,256]...) custom-call(s32[10]{0:T(128)S(1)} %pad_add_fusion.scalars, ...), custom_call_target="tpu_custom_call", output_to_operand_aliasing={{0}: (5, {}), {1}: (6, {}), {2}: (7, {}), {3}: (8, {}), {4}... | custom-call | tf_op jit(solution)/shard_map/recompute/pallas_call | solution.py:502
  18.4 4.5 %recompute.4 = (bf16[4,1920,256]{2,1,0:T(8,128)(2,1)S(1)}, bf16[32,256,80]{2,1,0:T(8,128)(2,1)S(1)}, bf16[32,256,256]{2,1,0:T(8,128)(2,1)S(1)}, bf16[4,1280,256]...) custom-call(s32[10]{0:T(128)S(1)} %pad_add_fusion.scalars, ...), custom_call_target="tpu_custom_call", output_to_operand_aliasing={{0}: (5, {}), {1}: (6, {}), {2}: (7, {}), {3}: (8, {}), {4}... | custom-call | tf_op jit(solution)/shard_map/recompute/pallas_call | solution.py:502
  24.2 4.5 %recompute.5 = (bf16[4,1920,256]{2,1,0:T(8,128)(2,1)S(1)}, bf16[32,256,80]{2,1,0:T(8,128)(2,1)S(1)}, bf16[32,256,256]{2,1,0:T(8,128)(2,1)S(1)}, bf16[4,1280,256]...) custom-call(s32[10]{0:T(128)S(1)} %pad_add_fusion.scalars, ...), custom_call_target="tpu_custom_call", output_to_operand_aliasing={{0}: (5, {}), {1}: (6, {}), {2}: (7, {}), {3}: (8, {}), {4}... | custom-call | tf_op jit(solution)/shard_map/recompute/pallas_call | solution.py:502
  30.6 1.3 collective-permute-start.5
  34.0 46.4 %collective-permute-done.5.refs_0_ = bf16[1280,256]{1,0:T(8,128)(2,1)S(1)} collective-permute-done((bf16[1280,256]{1,0:T(8,128)(2,1)S(1)}, bf16[1280,256]{1,0:T(8,128)(2,1)S(1)}, u32[]{:S(2)}, u32[]{:S(2)}) %collective-permute-start.5) | collective-permute-done | bytes 655392 | tf_op jit(solution)/shard_map/ppermute | solution.py:598
  80.4 2.8 %backward.15 = (bf16[1280,256]{1,0:T(8,128)(2,1)S(1)}, bf16[4,1920,256]{2,1,0:T(8,128)(2,1)S(1)}, bf16[4,1280,256]{2,1,0:T(8,128)(2,1)S(1)}) custom-call(s32[10]{0:T(128)S(1)} %pad_add_fusion.scalars, bf16[1280,256]{1,0:T(8,128)(2,1)S(1)} %collective-permute-done.5.refs_0_, ...), custom_call_target="tpu_custom_call", output_to_operand_aliasing={{1}: (10, {}), {2}: (11, {})} | custom-call | tf_op jit(solution)/shard_map/backward/pallas_call | solution.py:527
  83.3 1.3 collective-permute-start.7
  84.6 2.9 %weights.3 = (bf16[1280,960]{1,0:T(8,128)(2,1)S(1)}, bf16[1280,960]{1,0:T(8,128)(2,1)S(1)}, bf16[1280,640]{1,0:T(8,128)(2,1)S(1)}) custom-call(bf16[4,1280,256]{2,1,0:T(8,128)(2,1)S(1)} %get-tuple-element.163.hidden, bf16[4,640,256]{2,1,0:T(8,128)(2,1)S(1)} %get-tuple-element.162.attn.refs_1_, ...), custom_call_target="tpu_custom_call" | custom-call | tf_op jit(solution)/shard_map/weights/pallas_call | solution.py:552
  87.5 7.4 %collective-permute-done.4.refs_0_ = bf16[1280,256]{1,0:T(8,128)(2,1)S(1)} collective-permute-done((bf16[1280,256]{1,0:T(8,128)(2,1)S(1)}, bf16[1280,256]{1,0:T(8,128)(2,1)S(1)}, u32[]{:S(2)}, u32[]{:S(2)}) %collective-permute-start.4) | collective-permute-done | bytes 655392 | tf_op jit(solution)/shard_map/ppermute | solution.py:598
  94.9 2.8 %backward.16 = (bf16[1280,256]{1,0:T(8,128)(2,1)S(1)}, bf16[4,1920,256]{2,1,0:T(8,128)(2,1)S(1)}, bf16[4,1280,256]{2,1,0:T(8,128)(2,1)S(1)}) custom-call(s32[10]{0:T(128)S(1)} %pad_add_fusion.scalars, bf16[1280,256]{1,0:T(8,128)(2,1)S(1)} %collective-permute-done.4.refs_0_, ...), custom_call_target="tpu_custom_call", output_to_operand_aliasing={{1}: (10, {}), {2}: (11, {})} | custom-call | tf_op jit(solution)/shard_map/backward/pallas_call | solution.py:527
  97.8 1.3 collective-permute-start.6
  99.1 3.0 %weights.4 = (bf16[1280,960]{1,0:T(8,128)(2,1)S(1)}, bf16[1280,960]{1,0:T(8,128)(2,1)S(1)}, bf16[1280,640]{1,0:T(8,128)(2,1)S(1)}) custom-call(bf16[4,1280,256]{2,1,0:T(8,128)(2,1)S(1)} %get-tuple-element.163.hidden, bf16[4,640,256]{2,1,0:T(8,128)(2,1)S(1)} %get-tuple-element.162.attn.refs_1_, ...), custom_call_target="tpu_custom_call", output_to_operand_aliasing={{0}: (4, {}), {1}: (5, {}), {2}: (6, {})} | custom-call | tf_op jit(solution)/shard_map/weights/pallas_call | solution.py:552
  102.1 6.7 %collective-permute-done.7.refs_0_ = bf16[1280,256]{1,0:T(8,128)(2,1)S(1)} collective-permute-done((bf16[1280,256]{1,0:T(8,128)(2,1)S(1)}, bf16[1280,256]{1,0:T(8,128)(2,1)S(1)}, u32[]{:S(2)}, u32[]{:S(2)}) %collective-permute-start.7) | collective-permute-done | bytes 655392 | tf_op jit(solution)/shard_map/ppermute | solution.py:598
  108.8 2.8 %backward.17 = (bf16[4,1920,256]{2,1,0:T(8,128)(2,1)S(1)}, bf16[4,1280,256]{2,1,0:T(8,128)(2,1)S(1)}) custom-call(s32[10]{0:T(128)S(1)} %pad_add_fusion.scalars, bf16[1280,256]{1,0:T(8,128)(2,1)S(1)} %collective-permute-done.7.refs_0_, ...), custom_call_target="tpu_custom_call", output_to_operand_aliasing={{0}: (10, {}), {1}: (11, {})} | custom-call | tf_op jit(solution)/shard_map/backward/pallas_call | solution.py:527
  111.6 3.0 %weights.5 = (bf16[1280,960]{1,0:T(8,128)(2,1)S(1)}, bf16[1280,960]{1,0:T(8,128)(2,1)S(1)}, bf16[1280,640]{1,0:T(8,128)(2,1)S(1)}) custom-call(bf16[4,1280,256]{2,1,0:T(8,128)(2,1)S(1)} %get-tuple-element.163.hidden, bf16[4,640,256]{2,1,0:T(8,128)(2,1)S(1)} %get-tuple-element.162.attn.refs_1_, ...), custom_call_target="tpu_custom_call", output_to_operand_aliasing={{0}: (4, {}), {1}: (5, {}), {2}: (6, {})} | custom-call | tf_op jit(solution)/shard_map/weights/pallas_call | solution.py:552
  114.6 8.6 %collective-permute-done.6.refs_0_ = bf16[1280,256]{1,0:T(8,128)(2,1)S(1)} collective-permute-done((bf16[1280,256]{1,0:T(8,128)(2,1)S(1)}, bf16[1280,256]{1,0:T(8,128)(2,1)S(1)}, u32[]{:S(2)}, u32[]{:S(2)}) %collective-permute-start.6) | collective-permute-done | bytes 655392 | tf_op jit(solution)/shard_map/ppermute | solution.py:598
  123.2 2.1 %tail_out.1 = (bf16[4,160,640]{2,1,0:T(8,128)(2,1)S(1)}, bf16[4,160,640]{2,1,0:T(8,128)(2,1)S(1)}, bf16[4,1280,256]{2,1,0:T(8,128)(2,1)S(1)}) custom-call(s32[10]{0:T(128)S(1)} %pad_add_fusion.scalars, bf16[1280,256]{1,0:T(8,128)(2,1)S(1)} %collective-permute-done.6.refs_0_, ...), custom_call_target="tpu_custom_call", output_to_operand_aliasing={{2}: (4, {})} | custom-call | tf_op jit(solution)/shard_map/tail_out/pallas_call | solution.py:607
  125.4 4.0 %tail_qkv.2 = (bf16[4,160,960]{2,1,0:T(8,128)(2,1)S(1)}, bf16[4,160,960]{2,1,0:T(8,128)(2,1)S(1)}) custom-call(s32[10]{0:T(128)S(1)} %pad_add_fusion.scalars, bf16[640,1280]{1,0:T(8,128)(2,1)S(1)} %get-tuple-element.105.refs_1_.refs_2_.wo_t, bf16[4,1920,256]{2,1,0:T(8,128)(2,1)S(1)} %get-tuple-element.141.refs_4_.packed, ...), custom_call_target="tpu_custom_call" | custom-call | tf_op jit(solution)/shard_map/tail_qkv/pallas_call | solution.py:623
  130.2 4.3 %tail_qkv.3 = (bf16[4,160,960]{2,1,0:T(8,128)(2,1)S(1)}, bf16[4,160,960]{2,1,0:T(8,128)(2,1)S(1)}) custom-call(s32[10]{0:T(128)S(1)} %pad_add_fusion.scalars, bf16[640,1280]{1,0:T(8,128)(2,1)S(1)} %get-tuple-element.105.refs_1_.refs_2_.wo_t, bf16[4,1920,256]{2,1,0:T(8,128)(2,1)S(1)} %get-tuple-element.141.refs_4_.packed, ...), custom_call_target="tpu_custom_call" | custom-call | tf_op jit(solution)/shard_map/tail_qkv/pallas_call | solution.py:623
  134.9 1.6 collective-permute-start.9
  137.9 1.6 collective-permute-start.13
  140.0 12.1 %collective-permute-done.9.arrived = bf16[2,160,960]{2,1,0:T(8,128)(2,1)S(1)} collective-permute-done((bf16[2,160,960]{2,1,0:T(8,128)(2,1)S(1)}, bf16[2,160,960]{2,1,0:T(8,128)(2,1)S(1)}, u32[]{:S(2)}, u32[]{:S(2)}) %collective-permute-start.9) | collective-permute-done | bytes 614432 | tf_op jit(solution)/shard_map/ppermute | solution.py:569
  152.2 1.6 collective-permute-start.10
  153.8 1.8 %collective-permute-done.13.arrived = bf16[2,160,960]{2,1,0:T(8,128)(2,1)S(1)} collective-permute-done((bf16[2,160,960]{2,1,0:T(8,128)(2,1)S(1)}, bf16[2,160,960]{2,1,0:T(8,128)(2,1)S(1)}, u32[]{:S(2)}, u32[]{:S(2)}) %collective-permute-start.13) | collective-permute-done | bytes 614432 | tf_op jit(solution)/shard_map/ppermute | solution.py:569
  155.7 1.6 collective-permute-start.14
  157.8 3.0 %collective-permute-done.17.arrived = bf16[2,160,384]{2,1,0:T(8,128)(2,1)S(1)} collective-permute-done((bf16[2,160,384]{2,1,0:T(8,128)(2,1)S(1)}, bf16[2,160,384]{2,1,0:T(8,128)(2,1)S(1)}, u32[]{:S(2)}, u32[]{:S(2)}) %collective-permute-start.17) | collective-permute-done | bytes 245792 | tf_op jit(solution)/shard_map/ppermute | solution.py:569
  160.9 1.6 collective-permute-start.18
  162.5 6.2 %collective-permute-done.15.arrived = bf16[2,160,256]{2,1,0:T(8,128)(2,1)S(1)} collective-permute-done((bf16[2,160,256]{2,1,0:T(8,128)(2,1)S(1)}, bf16[2,160,256]{2,1,0:T(8,128)(2,1)S(1)}, u32[]{:S(2)}, u32[]{:S(2)}) %collective-permute-start.15) | collective-permute-done | bytes 163872 | tf_op jit(solution)/shard_map/ppermute | solution.py:569
  168.7 1.6 collective-permute-start.16
  170.3 2.9 %collective-permute-done.16.refs_5_ = bf16[1,160,256]{2,1,0:T(8,128)(2,1)S(1)} collective-permute-done((bf16[1,160,256]{2,1,0:T(8,128)(2,1)S(1)}, bf16[1,160,256]{2,1,0:T(8,128)(2,1)S(1)}, u32[]{:S(2)}, u32[]{:S(2)}) %collective-permute-start.16) | collective-permute-done | bytes 81952 | tf_op jit(solution)/shard_map/ppermute | solution.py:569
  173.2 1.4 finish.1
  (36 shorter events, 13.5 us)
Async XLA Ops:
  1.4 0.7 copy-start
  11.6 11.3 %collective-permute-start = (bf16[1280,256]{1,0:T(8,128)(2,1)S(1)}, bf16[1280,256]{1,0:T(8,128)(2,1)S(1)}, u32[]{:S(2)}, u32[]{:S(2)}) collective-permute-start(bf16[1280,256]{1,0:T(8,128)(2,1)S(1)} %get-tuple-element.136), channel_id=1, source_target_pairs={{24,16},{25,17},{26,18},{27,19},{28,20},{29,21},{30,22},{31,23}} | collective-permute-start | bytes 1966088 | tf_op jit(solution)/shard_map/ppermute | solution.py:598
  17.5 11.3 %collective-permute-start.1 = (bf16[1280,256]{1,0:T(8,128)(2,1)S(1)}, bf16[1280,256]{1,0:T(8,128)(2,1)S(1)}, u32[]{:S(2)}, u32[]{:S(2)}) collective-permute-start(bf16[1280,256]{1,0:T(8,128)(2,1)S(1)} %get-tuple-element.144), channel_id=1, source_target_pairs={{24,16},{25,17},{26,18},{27,19},{28,20},{29,21},{30,22},{31,23}} | collective-permute-start | bytes 1966088 | tf_op jit(solution)/shard_map/ppermute | solution.py:598
  23.5 6.5 %collective-permute-start.3 = (bf16[1280,256]{1,0:T(8,128)(2,1)S(1)}, bf16[1280,256]{1,0:T(8,128)(2,1)S(1)}, u32[]{:S(2)}, u32[]{:S(2)}) collective-permute-start(bf16[1280,256]{1,0:T(8,128)(2,1)S(1)} %get-tuple-element.150), channel_id=1, source_target_pairs={{16,8},{24,16},{17,9},{25,17},{18,10},{26,18},{19,11},{27,19},{20,... | collective-permute-start | bytes 1966088 | tf_op jit(solution)/shard_map/ppermute | solution.py:598
  29.3 2.6 %collective-permute-start.2 = (bf16[1280,256]{1,0:T(8,128)(2,1)S(1)}, bf16[1280,256]{1,0:T(8,128)(2,1)S(1)}, u32[]{:S(2)}, u32[]{:S(2)}) collective-permute-start(bf16[1280,256]{1,0:T(8,128)(2,1)S(1)} %get-tuple-element.149), channel_id=1, source_target_pairs={{16,8},{24,16},{17,9},{25,17},{18,10},{26,18},{19,11},{27,19},{20,... | collective-permute-start | bytes 1966088 | tf_op jit(solution)/shard_map/ppermute | solution.py:598
  30.6 49.8 %collective-permute-start.5 = (bf16[1280,256]{1,0:T(8,128)(2,1)S(1)}, bf16[1280,256]{1,0:T(8,128)(2,1)S(1)}, u32[]{:S(2)}, u32[]{:S(2)}) collective-permute-start(bf16[1280,256]{1,0:T(8,128)(2,1)S(1)} %get-tuple-element.156), channel_id=1, source_target_pairs={{8,0},{16,8},{9,1},{17,9},{10,2},{18,10},{11,3},{19,11},{12,4},{20... | collective-permute-start | bytes 1966088 | tf_op jit(solution)/shard_map/ppermute | solution.py:598
  32.7 62.2 %collective-permute-start.4 = (bf16[1280,256]{1,0:T(8,128)(2,1)S(1)}, bf16[1280,256]{1,0:T(8,128)(2,1)S(1)}, u32[]{:S(2)}, u32[]{:S(2)}) collective-permute-start(bf16[1280,256]{1,0:T(8,128)(2,1)S(1)} %get-tuple-element.155), channel_id=1, source_target_pairs={{8,0},{16,8},{9,1},{17,9},{10,2},{18,10},{11,3},{19,11},{12,4},{20... | collective-permute-start | bytes 1966088 | tf_op jit(solution)/shard_map/ppermute | solution.py:598
  83.3 25.5 %collective-permute-start.7 = (bf16[1280,256]{1,0:T(8,128)(2,1)S(1)}, bf16[1280,256]{1,0:T(8,128)(2,1)S(1)}, u32[]{:S(2)}, u32[]{:S(2)}) collective-permute-start(bf16[1280,256]{1,0:T(8,128)(2,1)S(1)} %get-tuple-element.164), channel_id=1, source_target_pairs={{8,0},{9,1},{10,2},{11,3},{12,4},{13,5},{14,6},{15,7}} | collective-permute-start | bytes 1966088 | tf_op jit(solution)/shard_map/ppermute | solution.py:598
  97.8 25.5 %collective-permute-start.6 = (bf16[1280,256]{1,0:T(8,128)(2,1)S(1)}, bf16[1280,256]{1,0:T(8,128)(2,1)S(1)}, u32[]{:S(2)}, u32[]{:S(2)}) collective-permute-start(bf16[1280,256]{1,0:T(8,128)(2,1)S(1)} %get-tuple-element.161), channel_id=1, source_target_pairs={{8,0},{9,1},{10,2},{11,3},{12,4},{13,5},{14,6},{15,7}} | collective-permute-start | bytes 1966088 | tf_op jit(solution)/shard_map/ppermute | solution.py:598
  125.3 4.7 %collective-permute-start.11 = (bf16[4,160,640]{2,1,0:T(8,128)(2,1)S(1)}, bf16[4,160,640]{2,1,0:T(8,128)(2,1)S(1)}, u32[]{:S(2)}, u32[]{:S(2)}) collective-permute-start(bf16[4,160,640]{2,1,0:T(8,128)(2,1)S(1)} %get-tuple-element.185), channel_id=1, source_target_pairs={{0,1},{1,0},{2,3},{3,2},{4,5},{5,4},{6,7},{7,6},{8,9},{9,8},{10,11... | collective-permute-start | bytes 2457608 | tf_op jit(solution)/shard_map/ppermute | solution.py:569
  129.4 5.2 %collective-permute-start.8 = (bf16[4,160,960]{2,1,0:T(8,128)(2,1)S(1)}, bf16[4,160,960]{2,1,0:T(8,128)(2,1)S(1)}, u32[]{:S(2)}, u32[]{:S(2)}) collective-permute-start(bf16[4,160,960]{2,1,0:T(8,128)(2,1)S(1)} %get-tuple-element.179), channel_id=1, source_target_pairs={{0,1},{1,0},{2,3},{3,2},{4,5},{5,4},{6,7},{7,6},{8,9},{9,8},{10,11... | collective-permute-start | bytes 3686408 | tf_op jit(solution)/shard_map/ppermute | solution.py:569
  134.5 3.1 %collective-permute-start.12 = (bf16[4,160,960]{2,1,0:T(8,128)(2,1)S(1)}, bf16[4,160,960]{2,1,0:T(8,128)(2,1)S(1)}, u32[]{:S(2)}, u32[]{:S(2)}) collective-permute-start(bf16[4,160,960]{2,1,0:T(8,128)(2,1)S(1)} %get-tuple-element.193), channel_id=1, source_target_pairs={{0,1},{1,0},{2,3},{3,2},{4,5},{5,4},{6,7},{7,6},{8,9},{9,8},{10,11... | collective-permute-start | bytes 3686408 | tf_op jit(solution)/shard_map/ppermute | solution.py:569
  134.9 17.2 %collective-permute-start.9 = (bf16[2,160,960]{2,1,0:T(8,128)(2,1)S(1)}, bf16[2,160,960]{2,1,0:T(8,128)(2,1)S(1)}, u32[]{:S(2)}, u32[]{:S(2)}) collective-permute-start(bf16[2,160,960]{2,1,0:T(8,128)(2,1)S(1)} %get-tuple-element.181), channel_id=1, source_target_pairs={{0,2},{1,3},{2,0},{3,1},{4,6},{5,7},{6,4},{7,5},{8,10},{9,11},{10,... | collective-permute-start | bytes 1843208 | tf_op jit(solution)/shard_map/ppermute | solution.py:569
  137.9 17.7 %collective-permute-start.13 = (bf16[2,160,960]{2,1,0:T(8,128)(2,1)S(1)}, bf16[2,160,960]{2,1,0:T(8,128)(2,1)S(1)}, u32[]{:S(2)}, u32[]{:S(2)}) collective-permute-start(bf16[2,160,960]{2,1,0:T(8,128)(2,1)S(1)} %get-tuple-element.195), channel_id=1, source_target_pairs={{0,4},{1,5},{2,6},{3,7},{4,0},{5,1},{6,2},{7,3},{8,12},{9,13},{10,... | collective-permute-start | bytes 1843208 | tf_op jit(solution)/shard_map/ppermute | solution.py:569
  139.5 21.4 %collective-permute-start.17 = (bf16[2,160,384]{2,1,0:T(8,128)(2,1)S(1)}, bf16[2,160,384]{2,1,0:T(8,128)(2,1)S(1)}, u32[]{:S(2)}, u32[]{:S(2)}) collective-permute-start(bf16[2,160,384]{2,1,0:T(8,128)(2,1)S(1)} %get-tuple-element.203), channel_id=1, source_target_pairs={{0,4},{1,5},{2,6},{3,7},{4,0},{5,1},{6,2},{7,3},{8,12},{9,13},{10,... | collective-permute-start | bytes 737288 | tf_op jit(solution)/shard_map/ppermute | solution.py:569
  152.2 21.0 %collective-permute-start.10 = (bf16[1,160,960]{2,1,0:T(8,128)(2,1)S(1)}, bf16[1,160,960]{2,1,0:T(8,128)(2,1)S(1)}, u32[]{:S(2)}, u32[]{:S(2)}) collective-permute-start(bf16[1,160,960]{2,1,0:T(8,128)(2,1)S(1)} %get-tuple-element.183), channel_id=1, source_target_pairs={{0,4},{1,5},{2,6},{3,7},{4,0},{5,1},{6,2},{7,3},{8,12},{9,13},{10,... | collective-permute-start | bytes 921608 | tf_op jit(solution)/shard_map/ppermute | solution.py:569
  155.7 17.5 %collective-permute-start.14 = (bf16[1,160,960]{2,1,0:T(8,128)(2,1)S(1)}, bf16[1,160,960]{2,1,0:T(8,128)(2,1)S(1)}, u32[]{:S(2)}, u32[]{:S(2)}) collective-permute-start(bf16[1,160,960]{2,1,0:T(8,128)(2,1)S(1)} %get-tuple-element.197), channel_id=1, source_target_pairs={{0,2},{1,3},{2,0},{3,1},{4,6},{5,7},{6,4},{7,5},{8,10},{9,11},{10,... | collective-permute-start | bytes 921608 | tf_op jit(solution)/shard_map/ppermute | solution.py:569
  157.3 11.4 %collective-permute-start.15 = (bf16[2,160,256]{2,1,0:T(8,128)(2,1)S(1)}, bf16[2,160,256]{2,1,0:T(8,128)(2,1)S(1)}, u32[]{:S(2)}, u32[]{:S(2)}) collective-permute-start(bf16[2,160,256]{2,1,0:T(8,128)(2,1)S(1)} %get-tuple-element.199), channel_id=1, source_target_pairs={{0,2},{1,3},{2,0},{3,1},{4,6},{5,7},{6,4},{7,5},{8,10},{9,11},{10,... | collective-permute-start | bytes 491528 | tf_op jit(solution)/shard_map/ppermute | solution.py:569
  160.9 12.3 %collective-permute-start.18 = (bf16[1,160,384]{2,1,0:T(8,128)(2,1)S(1)}, bf16[1,160,384]{2,1,0:T(8,128)(2,1)S(1)}, u32[]{:S(2)}, u32[]{:S(2)}) collective-permute-start(bf16[1,160,384]{2,1,0:T(8,128)(2,1)S(1)} %get-tuple-element.205), channel_id=1, source_target_pairs={{0,2},{1,3},{2,0},{3,1},{4,6},{5,7},{6,4},{7,5},{8,10},{9,11},{10,... | collective-permute-start | bytes 368648 | tf_op jit(solution)/shard_map/ppermute | solution.py:569
  168.7 4.5 %collective-permute-start.16 = (bf16[1,160,256]{2,1,0:T(8,128)(2,1)S(1)}, bf16[1,160,256]{2,1,0:T(8,128)(2,1)S(1)}, u32[]{:S(2)}, u32[]{:S(2)}) collective-permute-start(bf16[1,160,256]{2,1,0:T(8,128)(2,1)S(1)} %get-tuple-element.201), channel_id=1, source_target_pairs={{0,4},{1,5},{2,6},{3,7},{4,0},{5,1},{6,2},{7,3},{8,12},{9,13},{10,... | collective-permute-start | bytes 245768 | tf_op jit(solution)/shard_map/ppermute | solution.py:569
where the time goes:
time: 175 us
  waiting for transfers between devices  96.4 us (55%)
  Pallas kernels  56.7 us (32%)
  starting transfers between devices  19.3 us (11%)
    ppermute x8, waiting for transfers between devices, per_device(): in_flight[slot + 2] = lax.ppermute(passed, 'section', pairs)  69.1 us
    ppermute x11, waiting for transfers between devices, exchange(): return lax.ppermute(value, 'dp', pairs)  27.2 us
    pallas_call x3, Pallas kernels, recompute(): pl.pallas_call(functools.partial(recompute_body, position, sections), out...  13.6 us
    pallas_call x9, Pallas kernels, backward(): pl.pallas_call(functools.partial(backward_body, slot, sections, arriving...  12.1 us
    ppermute x11, starting transfers between devices, exchange(): return lax.ppermute(value, 'dp', pairs)  11.1 us
    pallas_call x1, Pallas kernels, recompute(): pl.pallas_call(functools.partial(first_body, sections), out_shape=(kept_o...  8.99 us
    pallas_call x3, Pallas kernels, weights_step(): pl.pallas_call(functools.partial(weights_body, index), out_shape=(kept_on...  8.98 us
    pallas_call x2, Pallas kernels, tail_half(): pl.pallas_call(functools.partial(tail_half_body, last_slot, sections, hal...  8.34 us
  transfers between devices with their start and end apart: 19, of which 10 were waited for; matrix products, arithmetic and copies ran while one was open for 0% of the time, Pallas kernels for 25%

commit v1 on v0

--- a/solution.py
+++ b/solution.py
@@ -7,12 +7,13 @@
 from jax.experimental.pallas import tpu as pltpu
 from jax.sharding import PartitionSpec as P
 
+
 HDIM = 80
 HEADS = 8
 EPSILON = 1e-06
 SCALE = HDIM ** (-0.5)
 LOG2_E = 1.4426950408889634
-HALF = HEADS // 2
+PIECES = (HEADS // 2 + 1, HEADS // 2 - 1)
 ROWS_AT_A_TIME = 128
 WIDTH_CHUNKS = 5
 
@@ -62,16 +63,21 @@
         return 0
 
     lax.fori_loop(0, (heads - 2) // 2, two_steps, 0)
-    second(heads - 1, 1)
-    third(heads - 2, 0)
-    third(heads - 1, 1)
+    final = heads - 1
+    if heads % 2:
+        third(final - 2, 0)
+        second(final - 1, 1)
+        first(final, 0)
+    second(final, final % 2)
+    third(final - 1, 1 - final % 2)
+    third(final, final % 2)
 
 
 def over_lanes(column, lanes):
     return jnp.concatenate([column] * (lanes // column.shape[1]), axis=1)
 
 
-def normalize(position, x_buf, gain, normed, hidden, inv_std, rows_hidden, unit_rows, inv_rows):
+def normalize(position, x_buf, gain, inv_std, rows_hidden, unit_rows, inv_rows):
     slots = x_buf.shape[0]
 
     def some_rows(i, _):
@@ -135,7 +141,7 @@
     staged(HEADS, score, soften, mix)
 
 
-def recompute_body(position, sections, scalars, x_hbm, own, gain, w_qkv, *refs, before_part=None):
+def recompute_at(position, sections, scalars, x_hbm, own, gain, w_qkv, refs, before_part=None):
     packed, values, probs, normed, hidden, attn, inv_std, masked, inputs = refs[-22:-13]
     rows_hidden, unit_rows, inv_rows, queries, keys, g_buf = refs[-13:-7]
     scores, halves, sems = refs[-7:-5], refs[-5:-3], refs[-3:]
@@ -145,16 +151,12 @@
     is_last = scalars[0] == sections - 1
     own_copy = pltpu.make_async_copy(own.at[position], g_buf, sems[1])
     x_buf = inputs.at[position % 2]
-    if position == 0:
-        copy = pltpu.make_async_copy(x_hbm.at[0, micro], x_buf, sems[0])
-        copy.start()
-        for part in before_part:
-            part.start()
-        copy.wait()
-    if position + 1 < micro_count:
-        following = pltpu.make_async_copy(
-            x_hbm.at[0, scalars[3 + position]], inputs.at[(position + 1) % 2], sems[2]
-        )
+    has_next = position + 1 < micro_count
+    next_micro = scalars[2 + jnp.minimum(position + 1, micro_count - 1)]
+    following = pltpu.make_async_copy(x_hbm.at[0, next_micro], inputs.at[(position + 1) % 2], sems[2])
+
+    @pl.when(has_next)
+    def _():
         following.start()
 
     @pl.when(is_last)
@@ -162,10 +164,10 @@
         own_copy.start()
 
     exclude_keys(count, queries, keys)
-    normalize(position, x_buf, gain, normed, hidden, inv_std, rows_hidden, unit_rows, inv_rows)
+    normalize(position, x_buf, gain, inv_std, rows_hidden, unit_rows, inv_rows)
     for part in range(3):
         if before_part is not None:
-            before_part[part].wait()
+            before_part(part)
         project(position, part, w_qkv, packed, values, queries, keys, rows_hidden)
         if part == 0:
             normed[position] = unit_rows[...].T
@@ -180,23 +182,55 @@
         ids = lax.broadcasted_iota(jnp.int32, turned.shape, 1)
         masked[position] = jnp.where(ids < count, turned.astype(F32), 0.0).astype(BF)
 
-    if position + 1 < micro_count:
+    @pl.when(has_next)
+    def _():
         following.wait()
 
 
-def first_body(sections, scalars, x_hbm, own, gain, wq_hbm, wo_hbm, *refs):
-    wq, wo_t, gain_t = refs[:3]
+def recompute_body(slot, sections, scalars, x_hbm, own, gain, w_qkv, *refs):
+    micro_count = refs[-22].shape[0]
+    position = slot + scalars[1] % 2
+
+    @pl.when(position < micro_count)
+    def _():
+        recompute_at(position, sections, scalars, x_hbm, own, gain, w_qkv, refs)
+
+
+def first_body(sections, scalars, x_hbm, own, gain_hbm, wq_hbm, wo_hbm, *refs):
+    wq, wo_t, gain_t, gain_row = refs[:4]
+    inputs = refs[-16]
     wo, part_sems = refs[-2:]
+    micro_count = own.shape[0]
     width = HEADS * HDIM
     parts = []
     for part in range(3):
         cols = pl.ds(part * width, width)
         parts.append(pltpu.make_async_copy(wq_hbm.at[0, :, cols], wq.at[:, cols], part_sems.at[part]))
     parts.append(pltpu.make_async_copy(wo_hbm.at[0], wo, part_sems.at[3]))
-    recompute_body(0, sections, scalars, x_hbm, own, gain, wq, *refs[3:-2], before_part=parts)
-    gain_t[...] = jnp.broadcast_to(gain[0:1, :], (gain_t.shape[1], gain.shape[1])).T
-    parts[3].wait()
-    wo_t[...] = wo[...].T
+    gain_copy = pltpu.make_async_copy(gain_hbm, gain_row, part_sems.at[4])
+    x_copy = pltpu.make_async_copy(x_hbm.at[0, scalars[2]], inputs.at[0], part_sems.at[5])
+    gain_copy.start()
+    x_copy.start()
+    for part in parts:
+        part.start()
+    gain_copy.wait()
+    x_copy.wait()
+
+    def one(position, _):
+        def before_part(part):
+            @pl.when(position == 0)
+            def _():
+                parts[part].wait()
+                if part == 1:
+                    gain_t[...] = jnp.broadcast_to(gain_row[0:1, :], (gain_t.shape[1], gain_row.shape[1])).T
+                if part == 2:
+                    parts[3].wait()
+                    wo_t[...] = wo[...].T
+
+        recompute_at(position, sections, scalars, x_hbm, own, gain_row, wq, refs[4:-2], before_part)
+        return 0
+
+    lax.fori_loop(0, jnp.minimum(1 + scalars[1] % 2, micro_count), one, 0)
 
 
 def heads_backward(position, start, heads, gattn, packed, values, probs, out, offsets, grads, halves):
@@ -240,6 +274,17 @@
         @pl.when(section != sections - 1)
         def _():
             masked[position] = arriving[...]
+
+
+def into_heads(wo_t, masked, position, gattn):
+    chunk = wo_t.shape[0] // 2
+
+    def some_rows(i, _):
+        rows = pl.ds(pl.multiple_of(i * chunk, 16), chunk)
+        gattn[rows, :] = contract(wo_t[rows, :], masked[position]).astype(BF)
+        return 0
+
+    lax.fori_loop(0, 2, some_rows, 0)
 
 
 def backward_body(slot, sections, has_arriving, passes, scalars, *refs):
@@ -257,7 +302,7 @@
     @pl.when(valid)
     def _():
         take_arriving(sections, section, arriving, position, masked)
-        gattn[...] = contract(wo_t[...], masked[position]).astype(BF)
+        into_heads(wo_t, masked, position, gattn)
         span = HEADS * HDIM
         heads_backward(
             position,
@@ -307,24 +352,36 @@
         lax.fori_loop(0, WIDTH_CHUNKS, finish, 0)
 
 
+def piece_rows(half):
+    return half * PIECES[0] * HDIM, PIECES[half] * HDIM
+
+
 def gather_half(source, half, compact):
     width = HEADS * HDIM
-    span = HALF * HDIM
+    start, span = piece_rows(half)
     for part in range(3):
-        at = part * width + half * span
+        at = part * width + start
         compact[part * span : (part + 1) * span, :] = source[at : at + span, :]
 
 
-def weights_body(index, hidden, attn, grad_packed, masked, *refs):
-    acc_out, compact = refs[-2:]
-    acc_qkv = refs[-4:-2]
+def weights_body(index, early, sections, scalars, *refs):
+    ahead = (scalars[0] == sections - 1) & (scalars[1] % 2 == 1)
+
+    @pl.when(ahead if early else jnp.logical_not(ahead))
+    def _():
+        weights_at(index, *refs)
+
+
+def weights_at(index, hidden, attn, grad_packed, masked, *refs):
+    compact = refs[-2:]
+    acc_qkv, acc_out = refs[-5:-3], refs[-3]
     width = hidden.shape[1]
     chunk = width // 5
 
     def some_width(i, _):
         rows = pl.ds(pl.multiple_of(i * chunk, 16), chunk)
         for half in range(2):
-            total = contract(hidden[index, rows, :], compact[half], (1, 1))
+            total = contract(hidden[index, rows, :], compact[half][...], (1, 1))
             if index > 0:
                 total = total + acc_qkv[half][rows, :].astype(F32)
             acc_qkv[half][rows, :] = total.astype(BF)
@@ -335,7 +392,7 @@
         return 0
 
     for half in range(2):
-        gather_half(grad_packed.at[index], half, compact.at[half])
+        gather_half(grad_packed.at[index], half, compact[half])
     lax.fori_loop(0, 5, some_width, 0)
 
 
@@ -344,7 +401,7 @@
 
     def one(j, target, to):
         at = pl.multiple_of((dp_index ^ j) * block, 16)
-        value = contract(left[pl.ds(at, block), :], right, (1, 1)) + acc[pl.ds(at, block), :].astype(F32)
+        value = contract(left[pl.ds(at, block), :], right[...], (1, 1)) + acc[pl.ds(at, block), :].astype(F32)
         target[to] = value.astype(BF)
 
     def two(i, _):
@@ -355,37 +412,34 @@
     lax.fori_loop(0, count, two, 0)
 
 
-def tail_out_body(slot, sections, has_arriving, scalars, *refs):
+def tail_out_body(scalars, masked, attn, acc_out, sent, kept):
+    last = masked.shape[0] - 1
+    blocks_out(scalars[1], masked.at[last], attn.at[last], acc_out, sent, kept)
+
+
+def tail_half_body(slot, sections, half, has_arriving, scalars, *refs):
     arriving = None
     if has_arriving:
         arriving, refs = refs[0], refs[1:]
-    attn, acc_out = refs[:2]
-    sent, kept, masked = refs[-3:]
+    wo_t, packed, values, probs, masked_in, hidden, acc_qkv, gp_all = refs[:8]
+    sent, kept = refs[-8 - (half == 0)], refs[-7 - (half == 0)]
+    masked = refs[-7] if half == 0 else masked_in
+    gattn, compact = refs[-6:-4]
+    grads, halves = refs[-4:-2], refs[-2:]
     section, position, valid, _ = placing(slot, sections, scalars, masked.shape[0])
     last = masked.shape[0] - 1
+    start, span = piece_rows(half)
 
     @pl.when(valid)
     def _():
-        take_arriving(sections, section, arriving, position, masked)
-
-    blocks_out(scalars[1], masked.at[last], attn[last], acc_out, sent, kept)
-
-
-def tail_half_body(slot, sections, half, scalars, wo_t, packed, values, probs, masked, hidden, acc_qkv, gp_all, *refs):
-    sent, kept, gattn, compact = refs[-8:-4]
-    grads, halves = refs[-4:-2], refs[-2:]
-    _, position, valid, _ = placing(slot, sections, scalars, masked.shape[0])
-    last = masked.shape[0] - 1
-    span = HALF * HDIM
-
-    @pl.when(valid)
-    def _():
-        rows = slice(half * span, (half + 1) * span)
+        if half == 0:
+            take_arriving(sections, section, arriving, position, masked)
+        rows = slice(start, start + span)
         gattn[rows, :] = contract(wo_t[rows, :], masked[position]).astype(BF)
         heads_backward(
             position,
-            half * HALF,
-            HALF,
+            half * PIECES[0],
+            PIECES[half],
             gattn,
             packed,
             values,
@@ -400,7 +454,7 @@
     def _():
         gather_half(gp_all.at[last], half, compact)
 
-    blocks_out(scalars[1], hidden.at[last], compact[...], acc_qkv, sent, kept)
+    blocks_out(scalars[1], hidden.at[last], compact, acc_qkv, sent, kept)
 
 
 def halve_out_body(split, keeps, sends, kept, arrived, *outs):
@@ -420,13 +474,13 @@
 
 def finish_body(split, *refs):
     qkv, out = refs[-2:]
-    span = HALF * HDIM
     width = HEADS * HDIM
     for half in range(2):
+        start, span = piece_rows(half)
         kept, arrived = refs[2 * half : 2 * half + 2]
         total = kept[0].astype(F32) + arrived[0].astype(F32)
         for part in range(3):
-            at = part * width + half * span
+            at = part * width + start
             qkv[:, at : at + span] = total[:, part * span : (part + 1) * span]
     for piece, cols in enumerate((slice(0, split), slice(split, out.shape[1]))):
         kept, arrived = refs[4 + 2 * piece : 6 + 2 * piece]
@@ -445,11 +499,11 @@
     micro_count, slots, width = cotangent.shape
     packed_width = qkv_weight.shape[2]
     head_width = out_weight.shape[2]
-    span = packed_width // 2
+    spans = [3 * heads * HDIM for heads in PIECES]
     block = width // dp_count
-    activations, cotangent, qkv_weight, out_weight = (
+    activations, cotangent, norm_gain, qkv_weight, out_weight = (
         pltpu.with_memory_space_constraint(x, pltpu.HBM)
-        for x in (activations, cotangent, qkv_weight, out_weight)
+        for x in (activations, cotangent, norm_gain, qkv_weight, out_weight)
     )
     scalars = jnp.concatenate([jnp.stack([section, dp_index]).astype(jnp.int32), arrival, counts[:, 0]])
 
@@ -480,27 +534,30 @@
     ]
     state = {}
 
-    def recompute(position, weights):
+    def recompute_first():
         outs = tuple(shapes[name] for name in RECOMPUTED)
-        if position == 0:
-            results = pl.pallas_call(
-                functools.partial(first_body, sections),
-                out_shape=(
-                    kept_on_chip(qkv_weight.shape[1:], BF),
-                    kept_on_chip((head_width, width), BF),
-                    kept_on_chip((width, 128), F32),
-                    *outs,
-                ),
-                in_specs=[SMEM, HBM, HBM, VMEM, HBM, HBM],
-                out_specs=(VMEM,) * (3 + len(outs)),
-                scratch_shapes=row_scratch + [pltpu.VMEM((width, head_width), BF), pltpu.SemaphoreType.DMA((4,))],
-                compiler_params=pltpu.CompilerParams(vmem_limit_bytes=SCRATCH["recompute_first"] << 10),
-                name="recompute_first",
-            )(scalars, activations, cotangent, norm_gain, qkv_weight, out_weight)
-            state.update(zip(RECOMPUTED, results[3:]))
-            return results[:3]
         results = pl.pallas_call(
-            functools.partial(recompute_body, position, sections),
+            functools.partial(first_body, sections),
+            out_shape=(
+                kept_on_chip(qkv_weight.shape[1:], BF),
+                kept_on_chip((head_width, width), BF),
+                kept_on_chip((width, 128), F32),
+                kept_on_chip(norm_gain.shape, F32),
+                *outs,
+            ),
+            in_specs=[SMEM, HBM, HBM, HBM, HBM, HBM],
+            out_specs=(VMEM,) * (4 + len(outs)),
+            scratch_shapes=row_scratch + [pltpu.VMEM((width, head_width), BF), pltpu.SemaphoreType.DMA((6,))],
+            compiler_params=pltpu.CompilerParams(vmem_limit_bytes=SCRATCH["recompute_first"] << 10),
+            name="recompute_first",
+        )(scalars, activations, cotangent, norm_gain, qkv_weight, out_weight)
+        state.update(zip(RECOMPUTED, results[4:]))
+        return results[:3], results[3]
+
+    def recompute(slot, gain, weights):
+        outs = tuple(shapes[name] for name in RECOMPUTED)
+        results = pl.pallas_call(
+            functools.partial(recompute_body, slot, sections),
             out_shape=outs,
             in_specs=[SMEM, HBM, HBM, VMEM, VMEM] + [ANY] * len(outs),
             out_specs=(VMEM,) * len(outs),
@@ -508,9 +565,8 @@
             input_output_aliases={5 + i: i for i in range(len(outs))},
             compiler_params=pltpu.CompilerParams(vmem_limit_bytes=SCRATCH["recompute"] << 10),
             name="recompute",
-        )(scalars, activations, cotangent, norm_gain, weights[0], *(state[name] for name in RECOMPUTED))
+        )(scalars, activations, cotangent, gain, weights[0], *(state[name] for name in RECOMPUTED))
         state.update(zip(RECOMPUTED, results))
-        return weights
 
     def backward(slot, arriving, weights, passes):
         extra = [] if arriving is None else [arriving]
@@ -541,24 +597,23 @@
         state.update(zip(COTANGENTS, results[-2:]))
         return results[0]
 
-    def weights_step(index):
-        operands = [state[name] for name in ("hidden", "attn", "grad_packed", "masked")]
-        specs = [VMEM] * len(operands)
+    def weights_step(index, early):
+        operands = [scalars, *(state[name] for name in ("hidden", "attn", "grad_packed", "masked"))]
+        specs = [SMEM] + [VMEM] * (len(operands) - 1)
         aliases = {}
-        if index > 0:
+        if "sums" in state:
             aliases = {len(operands) + i: i for i in range(3)}
             operands += state["sums"]
             specs += [ANY] * 3
         state["sums"] = pl.pallas_call(
-            functools.partial(weights_body, index),
+            functools.partial(weights_body, index, early, sections),
             out_shape=(
-                kept_on_chip((width, span), BF),
-                kept_on_chip((width, span), BF),
+                *(kept_on_chip((width, span), BF) for span in spans),
                 kept_on_chip((width, head_width), BF),
             ),
             in_specs=specs,
             out_specs=(VMEM,) * 3,
-            scratch_shapes=[pltpu.VMEM((2, span, slots), BF)],
+            scratch_shapes=[pltpu.VMEM((span, slots), BF) for span in spans],
             input_output_aliases=aliases,
             compiler_params=pltpu.CompilerParams(vmem_limit_bytes=SCRATCH["weights"] << 10),
             name="weights",
@@ -584,10 +639,13 @@
 
     last_slot = micro_count + 2 * (sections - 1) - 1
     in_flight = {}
-    weights = None
+    weights, gain = recompute_first()
     for slot in range(last_slot):
-        if slot < micro_count:
-            weights = recompute(slot, weights)
+        if 0 < slot < micro_count:
+            recompute(slot, gain, weights)
+        if slot == micro_count - 1:
+            for index in range(micro_count - 1):
+                weights_step(index, True)
         pairs = [
             (s, s - 1)
             for s in range(1, sections)
@@ -598,62 +656,58 @@
             in_flight[slot + 2] = lax.ppermute(passed, "section", pairs)
         index = slot - 2 * (sections - 1)
         if 0 <= index < micro_count - 1:
-            weights_step(index)
+            weights_step(index, False)
 
     arriving = in_flight.pop(last_slot, None)
-    extra = [] if arriving is None else [arriving]
     pair_shape = (dp_count // 2, block)
-    operands = [scalars, *extra, state["attn"], state["sums"][2], state["masked"]]
-    sent_out, kept_out, masked = pl.pallas_call(
-        functools.partial(tail_out_body, last_slot, sections, arriving is not None),
-        out_shape=(
-            jax.ShapeDtypeStruct((*pair_shape, head_width), BF),
-            jax.ShapeDtypeStruct((*pair_shape, head_width), BF),
-            shapes["masked"],
-        ),
-        in_specs=[SMEM] + [VMEM] * (len(operands) - 2) + [ANY],
-        out_specs=(VMEM,) * 3,
-        input_output_aliases={len(operands) - 1: 2},
-        compiler_params=pltpu.CompilerParams(vmem_limit_bytes=SCRATCH["tail_out"] << 10),
-        name="tail_out",
-    )(*operands)
-    arrived_out = exchange(sent_out, 1)
-
-    def tail_half(half, scalars):
-        sent, kept = pl.pallas_call(
-            functools.partial(tail_half_body, last_slot, sections, half),
-            out_shape=(
-                jax.ShapeDtypeStruct((*pair_shape, span), BF),
-                jax.ShapeDtypeStruct((*pair_shape, span), BF),
-            ),
-            in_specs=[SMEM] + [VMEM] * 8,
-            out_specs=(VMEM, VMEM),
-            scratch_shapes=[pltpu.VMEM((head_width, slots), BF), pltpu.VMEM((span, slots), BF), *head_scratch],
+
+    def tail_half(half, scalars, masked, arriving):
+        extra = [] if arriving is None else [arriving]
+        pair = jax.ShapeDtypeStruct((*pair_shape, spans[half]), BF)
+        operands = [scalars, *extra, weights[1], state["packed"], state["values"], state["probs"], masked]
+        at_masked = len(operands) - 1
+        operands += [state["hidden"], state["sums"][half], state["grad_packed"]]
+        specs = [SMEM] + [VMEM] * (len(operands) - 1)
+        if half == 0:
+            specs[at_masked] = ANY
+        results = pl.pallas_call(
+            functools.partial(tail_half_body, last_slot, sections, half, arriving is not None),
+            out_shape=(pair, pair, shapes["masked"]) if half == 0 else (pair, pair),
+            in_specs=specs,
+            out_specs=(VMEM,) * (3 if half == 0 else 2),
+            scratch_shapes=[pltpu.VMEM((head_width, slots), BF), pltpu.VMEM((spans[half], slots), BF), *head_scratch],
+            input_output_aliases={at_masked: 2} if half == 0 else {},
             compiler_params=pltpu.CompilerParams(vmem_limit_bytes=SCRATCH["tail_qkv"] << 10),
             name="tail_qkv",
-        )(
-            scalars,
-            weights[1],
-            state["packed"],
-            state["values"],
-            state["probs"],
-            masked,
-            state["hidden"],
-            state["sums"][half],
-            state["grad_packed"],
-        )
-        return kept, exchange(sent, 1)
+        )(*operands)
+        return results[1], exchange(results[0], 1), (results[2] if half == 0 else masked)
 
     bits = [1 << i for i in range(1, dp_count.bit_length() - 1)]
     held = list(range(0, dp_count, 2))
     split = head_width // 256 * 128
-    first = tail_half(0, scalars)
+    orders = [bits, bits[::-1]]
+    kept, arrived, masked = tail_half(0, scalars, state["masked"], arriving)
+    sent_out, kept_out = pl.pallas_call(
+        tail_out_body,
+        out_shape=(jax.ShapeDtypeStruct((*pair_shape, head_width), BF),) * 2,
+        in_specs=[SMEM] + [VMEM] * 3,
+        out_specs=(VMEM, VMEM),
+        compiler_params=pltpu.CompilerParams(vmem_limit_bytes=SCRATCH["tail_out"] << 10),
+        name="tail_out",
+    )(scalars, masked, state["attn"], state["sums"][2])
+    arrived_out = exchange(sent_out, 1)
+    kept, kept_out = lax.optimization_barrier((kept, kept_out))
+    first = halve(kept, arrived, orders[0][0], held)
+    later_scalars, first_kept = lax.optimization_barrier((scalars, first[0]))
+    first = (first_kept, *first[1:])
+    kept, arrived, _ = tail_half(1, later_scalars, masked, None)
     keeps = [[i for i, j in enumerate(held) if not j & bit] for bit in (bits[0], bits[-1])]
     sends = [[i for i, j in enumerate(held) if j & bit] for bit in (bits[0], bits[-1])]
     piece_shapes = [
         jax.ShapeDtypeStruct((len(held) // 2, block, cols), BF)
         for cols in (split, split, head_width - split, head_width - split)
     ]
+    kept, kept_out = lax.optimization_barrier((kept, kept_out))
     kept_a, sent_a, kept_b, sent_b = pl.pallas_call(
         functools.partial(halve_out_body, split, keeps, sends),
         out_shape=tuple(piece_shapes),
@@ -662,20 +716,18 @@
         compiler_params=pltpu.CompilerParams(vmem_limit_bytes=SCRATCH["halve_out"] << 10),
         name="halve_out",
     )(kept_out, arrived_out)
-    later_scalars, kept_a, sent_a, kept_b, sent_b = lax.optimization_barrier(
-        (scalars, kept_a, sent_a, kept_b, sent_b)
-    )
     out_streams = [
         (kept_a, exchange(sent_a, bits[0]), [held[i] for i in keeps[0]]),
         (kept_b, exchange(sent_b, bits[-1]), [held[i] for i in keeps[1]]),
     ]
-    second = tail_half(1, later_scalars)
-    orders = [bits, bits[::-1]]
-    qkv_streams = [(*first, held), (*second, held)]
-    for step in range(len(bits)):
-        if step > 0:
-            for i in range(2):
-                out_streams[i] = halve(*out_streams[i][:2], orders[i][step], out_streams[i][2])
+    second = halve(kept, arrived, orders[1][0], held)
+    qkv_streams = [first, second]
+    for step in range(1, len(bits)):
+        for i in range(2):
+            out_streams[i] = halve(*out_streams[i][:2], orders[i][step], out_streams[i][2])
+        waited = lax.optimization_barrier((qkv_streams[0][0], out_streams[0][0], out_streams[1][0]))
+        qkv_streams[0] = (waited[0], *qkv_streams[0][1:])
+        out_streams = [(waited[1 + i], *out_streams[i][1:]) for i in range(2)]
         for i in range(2):
             qkv_streams[i] = halve(*qkv_streams[i][:2], orders[i][step], qkv_streams[i][2])
     flat = [x for kept, arrived, _ in qkv_streams + out_streams for x in (kept, arrived)]

time: 175 us -> 171 us (0.977)
  waiting for transfers between devices: 96.4 us -> 90.8 us
  Pallas kernels: 56.7 us -> 59 us
    ppermute x8, waiting for transfers between devices: 69.1 us -> 63.1 us  [per_device(): in_flight[slot + 2] = lax.ppermute(passed, 'section', pairs)]
    pallas_call x8 -> x11, Pallas kernels: 33.6 us -> 35.4 us  [the longest x3 14 us: recompute(): pl.pallas_call(functools.partial(recompute_body, slot, sections), out_sha...]
  transfers between devices with their start and end apart: 19 -> 19, of which waited for: 10 -> 8; matrix products, arithmetic and copies ran while one was open for 0% -> 0% of each run, Pallas kernels for 25% -> 24%
where the time goes in v1:
time: 171 us
  waiting for transfers between devices  90.8 us (53%)
  Pallas kernels  59 us (35%)
  starting transfers between devices  19.7 us (12%)
    ppermute x8, waiting for transfers between devices, per_device(): in_flight[slot + 2] = lax.ppermute(passed, 'section', pairs)  63.1 us
    ppermute x11, waiting for transfers between devices, exchange(): return lax.ppermute(value, 'dp', pairs)  27.7 us
    pallas_call x3, Pallas kernels, recompute(): pl.pallas_call(functools.partial(recompute_body, slot, sections), out_sha...  14 us
    pallas_call x9, Pallas kernels, backward(): pl.pallas_call(functools.partial(backward_body, slot, sections, arriving...  12.9 us
    pallas_call x6, Pallas kernels, weights_step(): pl.pallas_call(functools.partial(weights_body, index, early, sections), o...  12.3 us
    ppermute x11, starting transfers between devices, exchange(): return lax.ppermute(value, 'dp', pairs)  11.7 us
    pallas_call x2, Pallas kernels, tail_half(): pl.pallas_call(functools.partial(tail_half_body, last_slot, sections, hal...  7.99 us
    ppermute x8, starting transfers between devices, per_device(): in_flight[slot + 2] = lax.ppermute(passed, 'section', pairs)  7.98 us
  transfers between devices with their start and end apart: 19, of which 8 were waited for; matrix products, arithmetic and copies ran while one was open for 0% of the time, Pallas kernels for 24%

profile of v1, /device:TPU:0, one launch (start us, length us, event | category | flops | bytes accessed | tf_op | source)
XLA Modules:
  0.0 171.2 jit_solution(1005058632509141261)
XLA Ops:
  1.4 7.1 %recompute_first.1 = (bf16[1280,1920]{1,0:T(8,128)(2,1)S(1)}, bf16[640,1280]{1,0:T(8,128)(2,1)S(1)}, f32[1280,128]{1,0:T(8,128)S(1)}, f32[1,1280]{1,0:T(1,128)S(...) custom-call(s32[10]{0:T(128)S(1)} %pad_add_fusion.scalars, ...), custom_call_target="tpu_custom_call" | custom-call | tf_op jit(solution)/shard_map/recompute_first/pallas_call | solution.py:539
  9.7 4.5 %recompute.3 = (bf16[4,1920,256]{2,1,0:T(8,128)(2,1)S(1)}, bf16[32,256,80]{2,1,0:T(8,128)(2,1)S(1)}, bf16[32,256,256]{2,1,0:T(8,128)(2,1)S(1)}, bf16[4,1280,256]...) custom-call(s32[10]{0:T(128)S(1)} %pad_add_fusion.scalars, ...), custom_call_target="tpu_custom_call", output_to_operand_aliasing={{0}: (5, {}), {1}: (6, {}), {2}: (7, {}), {3}: (8, {}), {4}... | custom-call | tf_op jit(solution)/shard_map/recompute/pallas_call | solution.py:559
  15.6 4.9 %recompute.4 = (bf16[4,1920,256]{2,1,0:T(8,128)(2,1)S(1)}, bf16[32,256,80]{2,1,0:T(8,128)(2,1)S(1)}, bf16[32,256,256]{2,1,0:T(8,128)(2,1)S(1)}, bf16[4,1280,256]...) custom-call(s32[10]{0:T(128)S(1)} %pad_add_fusion.scalars, ...), custom_call_target="tpu_custom_call", output_to_operand_aliasing={{0}: (5, {}), {1}: (6, {}), {2}: (7, {}), {3}: (8, {}), {4}... | custom-call | tf_op jit(solution)/shard_map/recompute/pallas_call | solution.py:559
  21.8 4.5 %recompute.5 = (bf16[4,1920,256]{2,1,0:T(8,128)(2,1)S(1)}, bf16[32,256,80]{2,1,0:T(8,128)(2,1)S(1)}, bf16[32,256,256]{2,1,0:T(8,128)(2,1)S(1)}, bf16[4,1280,256]...) custom-call(s32[10]{0:T(128)S(1)} %pad_add_fusion.scalars, ...), custom_call_target="tpu_custom_call", output_to_operand_aliasing={{0}: (5, {}), {1}: (6, {}), {2}: (7, {}), {3}: (8, {}), {4}... | custom-call | tf_op jit(solution)/shard_map/recompute/pallas_call | solution.py:559
  29.9 1.3 collective-permute-start.5
  31.8 1.3 collective-permute-start.4
  33.1 36.1 %collective-permute-done.5.refs_0_ = bf16[1280,256]{1,0:T(8,128)(2,1)S(1)} collective-permute-done((bf16[1280,256]{1,0:T(8,128)(2,1)S(1)}, bf16[1280,256]{1,0:T(8,128)(2,1)S(1)}, u32[]{:S(2)}, u32[]{:S(2)}) %collective-permute-start.5) | collective-permute-done | bytes 655392 | tf_op jit(solution)/shard_map/ppermute | solution.py:656
  69.2 3.3 %backward.15 = (bf16[1280,256]{1,0:T(8,128)(2,1)S(1)}, bf16[4,1920,256]{2,1,0:T(8,128)(2,1)S(1)}, bf16[4,1280,256]{2,1,0:T(8,128)(2,1)S(1)}) custom-call(s32[10]{0:T(128)S(1)} %pad_add_fusion.scalars, bf16[1280,256]{1,0:T(8,128)(2,1)S(1)} %collective-permute-done.5.refs_0_, ...), custom_call_target="tpu_custom_call", output_to_operand_aliasing={{1}: (10, {}), {2}: (11, {})} | custom-call | tf_op jit(solution)/shard_map/backward/pallas_call | solution.py:583
  72.6 1.3 collective-permute-start.7
  73.9 3.5 %weights.9 = (bf16[1280,1200]{1,0:T(8,128)(2,1)S(1)}, bf16[1280,720]{1,0:T(8,128)(2,1)S(1)}, bf16[1280,640]{1,0:T(8,128)(2,1)S(1)}) custom-call(s32[10]{0:T(128)S(1)} %pad_add_fusion.scalars, bf16[4,1280,256]{2,1,0:T(8,128)(2,1)S(1)} %get-tuple-element.181.refs_0_.refs_6_.refs_5_, ...), custom_call_target="tpu_custom_call", output_to_operand_aliasing={{0}: (5, {}), {1}: (6, {}), {2}: (7, {})} | custom-call | tf_op jit(solution)/shard_map/weights/pallas_call | solution.py:608
  77.4 10.1 %collective-permute-done.4.refs_0_ = bf16[1280,256]{1,0:T(8,128)(2,1)S(1)} collective-permute-done((bf16[1280,256]{1,0:T(8,128)(2,1)S(1)}, bf16[1280,256]{1,0:T(8,128)(2,1)S(1)}, u32[]{:S(2)}, u32[]{:S(2)}) %collective-permute-start.4) | collective-permute-done | bytes 655392 | tf_op jit(solution)/shard_map/ppermute | solution.py:656
  87.4 3.1 %backward.16 = (bf16[1280,256]{1,0:T(8,128)(2,1)S(1)}, bf16[4,1920,256]{2,1,0:T(8,128)(2,1)S(1)}, bf16[4,1280,256]{2,1,0:T(8,128)(2,1)S(1)}) custom-call(s32[10]{0:T(128)S(1)} %pad_add_fusion.scalars, bf16[1280,256]{1,0:T(8,128)(2,1)S(1)} %collective-permute-done.4.refs_0_, ...), custom_call_target="tpu_custom_call", output_to_operand_aliasing={{1}: (10, {}), {2}: (11, {})} | custom-call | tf_op jit(solution)/shard_map/backward/pallas_call | solution.py:583
  90.5 1.3 collective-permute-start.6
  91.8 3.6 %weights.10 = (bf16[1280,1200]{1,0:T(8,128)(2,1)S(1)}, bf16[1280,720]{1,0:T(8,128)(2,1)S(1)}, bf16[1280,640]{1,0:T(8,128)(2,1)S(1)}) custom-call(s32[10]{0:T(128)S(1)} %pad_add_fusion.scalars, bf16[4,1280,256]{2,1,0:T(8,128)(2,1)S(1)} %get-tuple-element.181.refs_0_.refs_6_.refs_5_, ...), custom_call_target="tpu_custom_call", output_to_operand_aliasing={{0}: (5, {}), {1}: (6, {}), {2}: (7, {})} | custom-call | tf_op jit(solution)/shard_map/weights/pallas_call | solution.py:608
  95.4 5.2 %collective-permute-done.7.refs_0_ = bf16[1280,256]{1,0:T(8,128)(2,1)S(1)} collective-permute-done((bf16[1280,256]{1,0:T(8,128)(2,1)S(1)}, bf16[1280,256]{1,0:T(8,128)(2,1)S(1)}, u32[]{:S(2)}, u32[]{:S(2)}) %collective-permute-start.7) | collective-permute-done | bytes 655392 | tf_op jit(solution)/shard_map/ppermute | solution.py:656
  100.6 3.1 %backward.17 = (bf16[4,1920,256]{2,1,0:T(8,128)(2,1)S(1)}, bf16[4,1280,256]{2,1,0:T(8,128)(2,1)S(1)}) custom-call(s32[10]{0:T(128)S(1)} %pad_add_fusion.scalars, bf16[1280,256]{1,0:T(8,128)(2,1)S(1)} %collective-permute-done.7.refs_0_, ...), custom_call_target="tpu_custom_call", output_to_operand_aliasing={{0}: (10, {}), {1}: (11, {})} | custom-call | tf_op jit(solution)/shard_map/backward/pallas_call | solution.py:583
  103.6 3.6 %weights.11 = (bf16[1280,1200]{1,0:T(8,128)(2,1)S(1)}, bf16[1280,720]{1,0:T(8,128)(2,1)S(1)}, bf16[1280,640]{1,0:T(8,128)(2,1)S(1)}) custom-call(s32[10]{0:T(128)S(1)} %pad_add_fusion.scalars, bf16[4,1280,256]{2,1,0:T(8,128)(2,1)S(1)} %get-tuple-element.181.refs_0_.refs_6_.refs_5_, ...), custom_call_target="tpu_custom_call", output_to_operand_aliasing={{0}: (5, {}), {1}: (6, {}), {2}: (7, {})} | custom-call | tf_op jit(solution)/shard_map/weights/pallas_call | solution.py:608
  107.2 11.8 %collective-permute-done.6.refs_0_ = bf16[1280,256]{1,0:T(8,128)(2,1)S(1)} collective-permute-done((bf16[1280,256]{1,0:T(8,128)(2,1)S(1)}, bf16[1280,256]{1,0:T(8,128)(2,1)S(1)}, u32[]{:S(2)}, u32[]{:S(2)}) %collective-permute-start.6) | collective-permute-done | bytes 655392 | tf_op jit(solution)/shard_map/ppermute | solution.py:656
  119.0 4.6 %tail_qkv.2 = (bf16[4,160,1200]{2,1,0:T(8,128)(2,1)S(1)}, bf16[4,160,1200]{2,1,0:T(8,128)(2,1)S(1)}, bf16[4,1280,256]{2,1,0:T(8,128)(2,1)S(1)}) custom-call(s32[10]{0:T(128)S(1)} %pad_add_fusion.scalars, bf16[1280,256]{1,0:T(8,128)(2,1)S(1)} %collective-permute-done.6.refs_0_, ...), custom_call_target="tpu_custom_call", output_to_operand_aliasing={{2}: (6, {})} | custom-call | tf_op jit(solution)/shard_map/tail_qkv/pallas_call | solution.py:673
  123.6 1.4 collective-permute-start.8
  125.0 2.0 %tail_out.1 = (bf16[4,160,640]{2,1,0:T(8,128)(2,1)S(1)}, bf16[4,160,640]{2,1,0:T(8,128)(2,1)S(1)}) custom-call(s32[10]{0:T(128)S(1)} %pad_add_fusion.scalars, bf16[4,1280,256]{2,1,0:T(8,128)(2,1)S(1)} %get-tuple-element.201.masked.refs_4_, bf16[4,640,256]{2,1,0:T(8,128)(2,1)S(1)} %get-tuple-element.182.refs_1_.attn, ...), custom_call_target="tpu_custom_call" | custom-call | tf_op jit(solution)/shard_map/tail_out/pallas_call | solution.py:690
  127.0 1.2 collective-permute-done.8.arrived
  128.5 3.4 %tail_qkv.3 = (bf16[4,160,720]{2,1,0:T(8,128)(2,1)S(1)}, bf16[4,160,720]{2,1,0:T(8,128)(2,1)S(1)}) custom-call(s32[10]{0:T(128)S(1)} %pad_add_fusion.scalars, bf16[640,1280]{1,0:T(8,128)(2,1)S(1)} %get-tuple-element.120.refs_1_.refs_2_.refs_0_, bf16[4,1920,256]{2,1,0:T(8,128)(2,1)S(1)} %get-tuple-element.157.refs_4_.refs_2_.refs_1_, ...), custom_call_target="tpu_custom_call" | custom-call | tf_op jit(solution)/shard_map/tail_qkv/pallas_call | solution.py:673
  132.5 1.5 collective-permute-start.12
  134.8 1.6 collective-permute-start.15
  136.6 0.9 collective-permute-start.11
  137.5 1.5 collective-permute-start.10
  139.0 17.5 %collective-permute-done.10.arrived = bf16[2,160,256]{2,1,0:T(8,128)(2,1)S(1)} collective-permute-done((bf16[2,160,256]{2,1,0:T(8,128)(2,1)S(1)}, bf16[2,160,256]{2,1,0:T(8,128)(2,1)S(1)}, u32[]{:S(2)}, u32[]{:S(2)}) %collective-permute-start.10) | collective-permute-done | bytes 163872 | tf_op jit(solution)/shard_map/ppermute | solution.py:624
  156.9 1.6 collective-permute-start.13
  158.6 1.6 collective-permute-start.16
  161.2 8.4 %collective-permute-done.17.refs_5_ = bf16[1,160,256]{2,1,0:T(8,128)(2,1)S(1)} collective-permute-done((bf16[1,160,256]{2,1,0:T(8,128)(2,1)S(1)}, bf16[1,160,256]{2,1,0:T(8,128)(2,1)S(1)}, u32[]{:S(2)}, u32[]{:S(2)}) %collective-permute-start.17) | collective-permute-done | bytes 81952 | tf_op jit(solution)/shard_map/ppermute | solution.py:624
  169.6 1.6 finish.1
  (37 shorter events, 12.0 us)
Async XLA Ops:
  9.0 11.5 %collective-permute-start.1 = (bf16[1280,256]{1,0:T(8,128)(2,1)S(1)}, bf16[1280,256]{1,0:T(8,128)(2,1)S(1)}, u32[]{:S(2)}, u32[]{:S(2)}) collective-permute-start(bf16[1280,256]{1,0:T(8,128)(2,1)S(1)} %get-tuple-element.152), channel_id=1, source_target_pairs={{24,16},{25,17},{26,18},{27,19},{28,20},{29,21},{30,22},{31,23}} | collective-permute-start | bytes 1966088 | tf_op jit(solution)/shard_map/ppermute | solution.py:656
  14.9 13.2 %collective-permute-start = (bf16[1280,256]{1,0:T(8,128)(2,1)S(1)}, bf16[1280,256]{1,0:T(8,128)(2,1)S(1)}, u32[]{:S(2)}, u32[]{:S(2)}) collective-permute-start(bf16[1280,256]{1,0:T(8,128)(2,1)S(1)} %get-tuple-element.140), channel_id=1, source_target_pairs={{24,16},{25,17},{26,18},{27,19},{28,20},{29,21},{30,22},{31,23}} | collective-permute-start | bytes 1966088 | tf_op jit(solution)/shard_map/ppermute | solution.py:656
  21.1 8.2 %collective-permute-start.3 = (bf16[1280,256]{1,0:T(8,128)(2,1)S(1)}, bf16[1280,256]{1,0:T(8,128)(2,1)S(1)}, u32[]{:S(2)}, u32[]{:S(2)}) collective-permute-start(bf16[1280,256]{1,0:T(8,128)(2,1)S(1)} %get-tuple-element.165), channel_id=1, source_target_pairs={{16,8},{24,16},{17,9},{25,17},{18,10},{26,18},{19,11},{27,19},{20,... | collective-permute-start | bytes 1966088 | tf_op jit(solution)/shard_map/ppermute | solution.py:656
  28.6 2.6 %collective-permute-start.2 = (bf16[1280,256]{1,0:T(8,128)(2,1)S(1)}, bf16[1280,256]{1,0:T(8,128)(2,1)S(1)}, u32[]{:S(2)}, u32[]{:S(2)}) collective-permute-start(bf16[1280,256]{1,0:T(8,128)(2,1)S(1)} %get-tuple-element.164), channel_id=1, source_target_pairs={{16,8},{24,16},{17,9},{25,17},{18,10},{26,18},{19,11},{27,19},{20,... | collective-permute-start | bytes 1966088 | tf_op jit(solution)/shard_map/ppermute | solution.py:656
  29.9 39.3 %collective-permute-start.5 = (bf16[1280,256]{1,0:T(8,128)(2,1)S(1)}, bf16[1280,256]{1,0:T(8,128)(2,1)S(1)}, u32[]{:S(2)}, u32[]{:S(2)}) collective-permute-start(bf16[1280,256]{1,0:T(8,128)(2,1)S(1)} %get-tuple-element.171), channel_id=1, source_target_pairs={{8,0},{16,8},{9,1},{17,9},{10,2},{18,10},{11,3},{19,11},{12,4},{20... | collective-permute-start | bytes 1966088 | tf_op jit(solution)/shard_map/ppermute | solution.py:656
  31.8 55.6 %collective-permute-start.4 = (bf16[1280,256]{1,0:T(8,128)(2,1)S(1)}, bf16[1280,256]{1,0:T(8,128)(2,1)S(1)}, u32[]{:S(2)}, u32[]{:S(2)}) collective-permute-start(bf16[1280,256]{1,0:T(8,128)(2,1)S(1)} %get-tuple-element.170), channel_id=1, source_target_pairs={{8,0},{16,8},{9,1},{17,9},{10,2},{18,10},{11,3},{19,11},{12,4},{20... | collective-permute-start | bytes 1966088 | tf_op jit(solution)/shard_map/ppermute | solution.py:656
  72.6 28.0 %collective-permute-start.7 = (bf16[1280,256]{1,0:T(8,128)(2,1)S(1)}, bf16[1280,256]{1,0:T(8,128)(2,1)S(1)}, u32[]{:S(2)}, u32[]{:S(2)}) collective-permute-start(bf16[1280,256]{1,0:T(8,128)(2,1)S(1)} %get-tuple-element.177), channel_id=1, source_target_pairs={{8,0},{9,1},{10,2},{11,3},{12,4},{13,5},{14,6},{15,7}} | collective-permute-start | bytes 1966088 | tf_op jit(solution)/shard_map/ppermute | solution.py:656
  90.5 28.5 %collective-permute-start.6 = (bf16[1280,256]{1,0:T(8,128)(2,1)S(1)}, bf16[1280,256]{1,0:T(8,128)(2,1)S(1)}, u32[]{:S(2)}, u32[]{:S(2)}) collective-permute-start(bf16[1280,256]{1,0:T(8,128)(2,1)S(1)} %get-tuple-element.176), channel_id=1, source_target_pairs={{8,0},{9,1},{10,2},{11,3},{12,4},{13,5},{14,6},{15,7}} | collective-permute-start | bytes 1966088 | tf_op jit(solution)/shard_map/ppermute | solution.py:656
  123.6 4.6 %collective-permute-start.8 = (bf16[4,160,1200]{2,1,0:T(8,128)(2,1)S(1)}, bf16[4,160,1200]{2,1,0:T(8,128)(2,1)S(1)}, u32[]{:S(2)}, u32[]{:S(2)}) collective-permute-start(bf16[4,160,1200]{2,1,0:T(8,128)(2,1)S(1)} %get-tuple-element.205), channel_id=1, source_target_pairs={{0,1},{1,0},{2,3},{3,2},{4,5},{5,4},{6,7},{7,6},{8,9},{9,8},{10,11... | collective-permute-start | bytes 4608008 | tf_op jit(solution)/shard_map/ppermute | solution.py:624
  131.9 2.6 %collective-permute-start.14 = (bf16[4,160,720]{2,1,0:T(8,128)(2,1)S(1)}, bf16[4,160,720]{2,1,0:T(8,128)(2,1)S(1)}, u32[]{:S(2)}, u32[]{:S(2)}) collective-permute-start(bf16[4,160,720]{2,1,0:T(8,128)(2,1)S(1)} %get-tuple-element.225), channel_id=1, source_target_pairs={{0,1},{1,0},{2,3},{3,2},{4,5},{5,4},{6,7},{7,6},{8,9},{9,8},{10,11... | collective-permute-start | bytes 2764808 | tf_op jit(solution)/shard_map/ppermute | solution.py:624
  132.4 4.0 %collective-permute-start.9 = (bf16[4,160,640]{2,1,0:T(8,128)(2,1)S(1)}, bf16[4,160,640]{2,1,0:T(8,128)(2,1)S(1)}, u32[]{:S(2)}, u32[]{:S(2)}) collective-permute-start(bf16[4,160,640]{2,1,0:T(8,128)(2,1)S(1)} %get-tuple-element.213), channel_id=1, source_target_pairs={{0,1},{1,0},{2,3},{3,2},{4,5},{5,4},{6,7},{7,6},{8,9},{9,8},{10,11... | collective-permute-start | bytes 2457608 | tf_op jit(solution)/shard_map/ppermute | solution.py:624
  132.5 24.2 %collective-permute-start.12 = (bf16[2,160,1200]{2,1,0:T(8,128)(2,1)S(1)}, bf16[2,160,1200]{2,1,0:T(8,128)(2,1)S(1)}, u32[]{:S(2)}, u32[]{:S(2)}) collective-permute-start(bf16[2,160,1200]{2,1,0:T(8,128)(2,1)S(1)} %get-tuple-element.221), channel_id=1, source_target_pairs={{0,2},{1,3},{2,0},{3,1},{4,6},{5,7},{6,4},{7,5},{8,10},{9,11},{10,... | collective-permute-start | bytes 2304008 | tf_op jit(solution)/shard_map/ppermute | solution.py:624
  134.8 23.7 %collective-permute-start.15 = (bf16[2,160,720]{2,1,0:T(8,128)(2,1)S(1)}, bf16[2,160,720]{2,1,0:T(8,128)(2,1)S(1)}, u32[]{:S(2)}, u32[]{:S(2)}) collective-permute-start(bf16[2,160,720]{2,1,0:T(8,128)(2,1)S(1)} %get-tuple-element.227), channel_id=1, source_target_pairs={{0,4},{1,5},{2,6},{3,7},{4,0},{5,1},{6,2},{7,3},{8,12},{9,13},{10,... | collective-permute-start | bytes 1382408 | tf_op jit(solution)/shard_map/ppermute | solution.py:624
  136.6 20.0 %collective-permute-start.11 = (bf16[2,160,384]{2,1,0:T(8,128)(2,1)S(1)}, bf16[2,160,384]{2,1,0:T(8,128)(2,1)S(1)}, u32[]{:S(2)}, u32[]{:S(2)}) collective-permute-start(bf16[2,160,384]{2,1,0:T(8,128)(2,1)S(1)} %get-tuple-element.218), channel_id=1, source_target_pairs={{0,4},{1,5},{2,6},{3,7},{4,0},{5,1},{6,2},{7,3},{8,12},{9,13},{10,... | collective-permute-start | bytes 737288 | tf_op jit(solution)/shard_map/ppermute | solution.py:624
  137.5 19.0 %collective-permute-start.10 = (bf16[2,160,256]{2,1,0:T(8,128)(2,1)S(1)}, bf16[2,160,256]{2,1,0:T(8,128)(2,1)S(1)}, u32[]{:S(2)}, u32[]{:S(2)}) collective-permute-start(bf16[2,160,256]{2,1,0:T(8,128)(2,1)S(1)} %get-tuple-element.215), channel_id=1, source_target_pairs={{0,2},{1,3},{2,0},{3,1},{4,6},{5,7},{6,4},{7,5},{8,10},{9,11},{10,... | collective-permute-start | bytes 491528 | tf_op jit(solution)/shard_map/ppermute | solution.py:624
  156.9 12.7 %collective-permute-start.13 = (bf16[1,160,1200]{2,1,0:T(8,128)(2,1)S(1)}, bf16[1,160,1200]{2,1,0:T(8,128)(2,1)S(1)}, u32[]{:S(2)}, u32[]{:S(2)}) collective-permute-start(bf16[1,160,1200]{2,1,0:T(8,128)(2,1)S(1)} %get-tuple-element.223), channel_id=1, source_target_pairs={{0,4},{1,5},{2,6},{3,7},{4,0},{5,1},{6,2},{7,3},{8,12},{9,13},{10,... | collective-permute-start | bytes 1152008 | tf_op jit(solution)/shard_map/ppermute | solution.py:624
  158.6 11.0 %collective-permute-start.16 = (bf16[1,160,720]{2,1,0:T(8,128)(2,1)S(1)}, bf16[1,160,720]{2,1,0:T(8,128)(2,1)S(1)}, u32[]{:S(2)}, u32[]{:S(2)}) collective-permute-start(bf16[1,160,720]{2,1,0:T(8,128)(2,1)S(1)} %get-tuple-element.229), channel_id=1, source_target_pairs={{0,2},{1,3},{2,0},{3,1},{4,6},{5,7},{6,4},{7,5},{8,10},{9,11},{10,... | collective-permute-start | bytes 691208 | tf_op jit(solution)/shard_map/ppermute | solution.py:624
  160.1 9.5 %collective-permute-start.18 = (bf16[1,160,384]{2,1,0:T(8,128)(2,1)S(1)}, bf16[1,160,384]{2,1,0:T(8,128)(2,1)S(1)}, u32[]{:S(2)}, u32[]{:S(2)}) collective-permute-start(bf16[1,160,384]{2,1,0:T(8,128)(2,1)S(1)} %get-tuple-element.233), channel_id=1, source_target_pairs={{0,2},{1,3},{2,0},{3,1},{4,6},{5,7},{6,4},{7,5},{8,10},{9,11},{10,... | collective-permute-start | bytes 368648 | tf_op jit(solution)/shard_map/ppermute | solution.py:624
  160.7 8.9 %collective-permute-start.17 = (bf16[1,160,256]{2,1,0:T(8,128)(2,1)S(1)}, bf16[1,160,256]{2,1,0:T(8,128)(2,1)S(1)}, u32[]{:S(2)}, u32[]{:S(2)}) collective-permute-start(bf16[1,160,256]{2,1,0:T(8,128)(2,1)S(1)} %get-tuple-element.231), channel_id=1, source_target_pairs={{0,4},{1,5},{2,6},{3,7},{4,0},{5,1},{6,2},{7,3},{8,12},{9,13},{10,... | collective-permute-start | bytes 245768 | tf_op jit(solution)/shard_map/ppermute | solution.py:624

commit v2 on v1

--- a/solution.py
+++ b/solution.py
@@ -15,7 +15,7 @@
 LOG2_E = 1.4426950408889634
 PIECES = (HEADS // 2 + 1, HEADS // 2 - 1)
 ROWS_AT_A_TIME = 128
-WIDTH_CHUNKS = 5
+WIDTH_CHUNKS = 2
 
 BF = jnp.bfloat16
 F32 = jnp.float32
@@ -26,7 +26,7 @@
 SCRATCH = {
     "recompute_first": 8192,
     "recompute": 6144,
-    "backward": 5120,
+    "backward": 7168,
     "weights": 3072,
     "tail_out": 3072,
     "tail_qkv": 3072,
@@ -187,9 +187,13 @@
         following.wait()
 
 
+def runs_ahead(scalars):
+    return 1 - scalars[1] % 2
+
+
 def recompute_body(slot, sections, scalars, x_hbm, own, gain, w_qkv, *refs):
     micro_count = refs[-22].shape[0]
-    position = slot + scalars[1] % 2
+    position = slot + runs_ahead(scalars)
 
     @pl.when(position < micro_count)
     def _():
@@ -230,7 +234,7 @@
         recompute_at(position, sections, scalars, x_hbm, own, gain_row, wq, refs[4:-2], before_part)
         return 0
 
-    lax.fori_loop(0, jnp.minimum(1 + scalars[1] % 2, micro_count), one, 0)
+    lax.fori_loop(0, jnp.minimum(1 + runs_ahead(scalars), micro_count), one, 0)
 
 
 def heads_backward(position, start, heads, gattn, packed, values, probs, out, offsets, grads, halves):
@@ -277,14 +281,14 @@
 
 
 def into_heads(wo_t, masked, position, gattn):
-    chunk = wo_t.shape[0] // 2
+    chunk = wo_t.shape[0] // 4
 
     def some_rows(i, _):
         rows = pl.ds(pl.multiple_of(i * chunk, 16), chunk)
         gattn[rows, :] = contract(wo_t[rows, :], masked[position]).astype(BF)
         return 0
 
-    lax.fori_loop(0, 2, some_rows, 0)
+    lax.fori_loop(0, 4, some_rows, 0)
 
 
 def backward_body(slot, sections, has_arriving, passes, scalars, *refs):
@@ -342,14 +346,16 @@
         shown = lax.broadcasted_iota(jnp.int32, (1, slots), 1) < count
         inv = jnp.where(shown, inv_std[position, 0:1, :], 0.0)
 
+        piece = width // 5
+
         def finish(i, _):
-            rows = pl.ds(pl.multiple_of(i * chunk, 16), chunk)
+            rows = pl.ds(pl.multiple_of(i * piece, 16), piece)
             unit = normed[position, rows, :].astype(F32)
             grad_ln = inv * (grad_hidden[rows, :] - mean - unit * along)
             passed[rows, :] = (masked[position, rows, :].astype(F32) + grad_ln).astype(BF)
             return 0
 
-        lax.fori_loop(0, WIDTH_CHUNKS, finish, 0)
+        lax.fori_loop(0, 5, finish, 0)
 
 
 def piece_rows(half):
@@ -364,15 +370,7 @@
         compact[part * span : (part + 1) * span, :] = source[at : at + span, :]
 
 
-def weights_body(index, early, sections, scalars, *refs):
-    ahead = (scalars[0] == sections - 1) & (scalars[1] % 2 == 1)
-
-    @pl.when(ahead if early else jnp.logical_not(ahead))
-    def _():
-        weights_at(index, *refs)
-
-
-def weights_at(index, hidden, attn, grad_packed, masked, *refs):
+def weights_body(index, hidden, attn, grad_packed, masked, *refs):
     compact = refs[-2:]
     acc_qkv, acc_out = refs[-5:-3], refs[-3]
     width = hidden.shape[1]
@@ -457,14 +455,6 @@
     blocks_out(scalars[1], hidden.at[last], compact, acc_qkv, sent, kept)
 
 
-def halve_out_body(split, keeps, sends, kept, arrived, *outs):
-    for piece, cols in enumerate((slice(0, split), slice(split, kept.shape[2]))):
-        kept_out, sent_out = outs[2 * piece : 2 * piece + 2]
-        for target, sources in ((kept_out, keeps[piece]), (sent_out, sends[piece])):
-            for j, source in enumerate(sources):
-                target[j] = (kept[source, :, cols].astype(F32) + arrived[source, :, cols].astype(F32)).astype(BF)
-
-
 def halve_body(keeps, sends, kept, arrived, kept_out, sent_out):
     for j, source in enumerate(keeps):
         kept_out[j] = (kept[source].astype(F32) + arrived[source].astype(F32)).astype(BF)
@@ -472,7 +462,7 @@
         sent_out[j] = (kept[source].astype(F32) + arrived[source].astype(F32)).astype(BF)
 
 
-def finish_body(split, *refs):
+def finish_body(*refs):
     qkv, out = refs[-2:]
     width = HEADS * HDIM
     for half in range(2):
@@ -482,9 +472,8 @@
         for part in range(3):
             at = part * width + start
             qkv[:, at : at + span] = total[:, part * span : (part + 1) * span]
-    for piece, cols in enumerate((slice(0, split), slice(split, out.shape[1]))):
-        kept, arrived = refs[4 + 2 * piece : 6 + 2 * piece]
-        out[:, cols] = kept[0].astype(F32) + arrived[0].astype(F32)
+    kept, arrived = refs[4:6]
+    out[...] = kept[0].astype(F32) + arrived[0].astype(F32)
 
 
 def kept_on_chip(shape, dtype):
@@ -597,16 +586,16 @@
         state.update(zip(COTANGENTS, results[-2:]))
         return results[0]
 
-    def weights_step(index, early):
-        operands = [scalars, *(state[name] for name in ("hidden", "attn", "grad_packed", "masked"))]
-        specs = [SMEM] + [VMEM] * (len(operands) - 1)
+    def weights_step(index):
+        operands = [state[name] for name in ("hidden", "attn", "grad_packed", "masked")]
+        specs = [VMEM] * len(operands)
         aliases = {}
         if "sums" in state:
             aliases = {len(operands) + i: i for i in range(3)}
             operands += state["sums"]
             specs += [ANY] * 3
         state["sums"] = pl.pallas_call(
-            functools.partial(weights_body, index, early, sections),
+            functools.partial(weights_body, index),
             out_shape=(
                 *(kept_on_chip((width, span), BF) for span in spans),
                 kept_on_chip((width, head_width), BF),
@@ -643,9 +632,6 @@
     for slot in range(last_slot):
         if 0 < slot < micro_count:
             recompute(slot, gain, weights)
-        if slot == micro_count - 1:
-            for index in range(micro_count - 1):
-                weights_step(index, True)
         pairs = [
             (s, s - 1)
             for s in range(1, sections)
@@ -656,7 +642,7 @@
             in_flight[slot + 2] = lax.ppermute(passed, "section", pairs)
         index = slot - 2 * (sections - 1)
         if 0 <= index < micro_count - 1:
-            weights_step(index, False)
+            weights_step(index)
 
     arriving = in_flight.pop(last_slot, None)
     pair_shape = (dp_count // 2, block)
@@ -684,7 +670,6 @@
 
     bits = [1 << i for i in range(1, dp_count.bit_length() - 1)]
     held = list(range(0, dp_count, 2))
-    split = head_width // 256 * 128
     orders = [bits, bits[::-1]]
     kept, arrived, masked = tail_half(0, scalars, state["masked"], arriving)
     sent_out, kept_out = pl.pallas_call(
@@ -698,41 +683,23 @@
     arrived_out = exchange(sent_out, 1)
     kept, kept_out = lax.optimization_barrier((kept, kept_out))
     first = halve(kept, arrived, orders[0][0], held)
-    later_scalars, first_kept = lax.optimization_barrier((scalars, first[0]))
-    first = (first_kept, *first[1:])
+    kept_out, first_kept = lax.optimization_barrier((kept_out, first[0]))
+    third = halve(kept_out, arrived_out, orders[1][0], held)
+    later_scalars, third_kept = lax.optimization_barrier((scalars, third[0]))
+    first, third = (first_kept, *first[1:]), (third_kept, *third[1:])
     kept, arrived, _ = tail_half(1, later_scalars, masked, None)
-    keeps = [[i for i, j in enumerate(held) if not j & bit] for bit in (bits[0], bits[-1])]
-    sends = [[i for i, j in enumerate(held) if j & bit] for bit in (bits[0], bits[-1])]
-    piece_shapes = [
-        jax.ShapeDtypeStruct((len(held) // 2, block, cols), BF)
-        for cols in (split, split, head_width - split, head_width - split)
-    ]
-    kept, kept_out = lax.optimization_barrier((kept, kept_out))
-    kept_a, sent_a, kept_b, sent_b = pl.pallas_call(
-        functools.partial(halve_out_body, split, keeps, sends),
-        out_shape=tuple(piece_shapes),
-        in_specs=[VMEM, VMEM],
-        out_specs=(VMEM,) * 4,
-        compiler_params=pltpu.CompilerParams(vmem_limit_bytes=SCRATCH["halve_out"] << 10),
-        name="halve_out",
-    )(kept_out, arrived_out)
-    out_streams = [
-        (kept_a, exchange(sent_a, bits[0]), [held[i] for i in keeps[0]]),
-        (kept_b, exchange(sent_b, bits[-1]), [held[i] for i in keeps[1]]),
-    ]
     second = halve(kept, arrived, orders[1][0], held)
-    qkv_streams = [first, second]
+    streams = [first, second, third]
     for step in range(1, len(bits)):
-        for i in range(2):
-            out_streams[i] = halve(*out_streams[i][:2], orders[i][step], out_streams[i][2])
-        waited = lax.optimization_barrier((qkv_streams[0][0], out_streams[0][0], out_streams[1][0]))
-        qkv_streams[0] = (waited[0], *qkv_streams[0][1:])
-        out_streams = [(waited[1 + i], *out_streams[i][1:]) for i in range(2)]
-        for i in range(2):
-            qkv_streams[i] = halve(*qkv_streams[i][:2], orders[i][step], qkv_streams[i][2])
-    flat = [x for kept, arrived, _ in qkv_streams + out_streams for x in (kept, arrived)]
+        streams[2] = halve(*streams[2][:2], orders[1][step], streams[2][2])
+        waited = lax.optimization_barrier((streams[0][0], streams[2][0]))
+        streams[0] = (waited[0], *streams[0][1:])
+        streams[2] = (waited[1], *streams[2][1:])
+        streams[0] = halve(*streams[0][:2], orders[0][step], streams[0][2])
+        streams[1] = halve(*streams[1][:2], orders[1][step], streams[1][2])
+    flat = [x for kept, arrived, _ in streams for x in (kept, arrived)]
     qkv_share, out_share = pl.pallas_call(
-        functools.partial(finish_body, split),
+        finish_body,
         out_shape=(
             jax.ShapeDtypeStruct((block, packed_width), F32),
             jax.ShapeDtypeStruct((block, head_width), F32),

time: 171 us -> 166 us (0.971)
  starting transfers between devices: 19.7 us -> 16.7 us
  Pallas kernels: 59 us -> 57.2 us
    pallas_call x1, Pallas kernels: 7.06 us -> 11.7 us  [recompute_first(): pl.pallas_call(functools.partial(first_body, sections), out_shape=(kept_o...]
    pallas_call x3, Pallas kernels: 14 us -> 10.1 us  [recompute(): pl.pallas_call(functools.partial(recompute_body, slot, sections), out_sha...]
    pallas_call x8 -> x4, Pallas kernels: 14.1 us -> 10.5 us  [the longest x3 8.92 us: weights_step(): pl.pallas_call(functools.partial(weights_body, index), out_shape=(*(kept_...]
    ppermute x11 -> x9, starting transfers between devices: 11.7 us -> 8.51 us  [exchange(): return lax.ppermute(value, 'dp', pairs)]
    ppermute x11 -> x9, waiting for transfers between devices: 27.7 us -> 28.5 us  [exchange(): return lax.ppermute(value, 'dp', pairs)]
  transfers between devices with their start and end apart: 19 -> 17, of which waited for: 8 -> 10; matrix products, arithmetic and copies ran while one was open for 0% -> 0% of each run, Pallas kernels for 24% -> 21%
where the time goes in v2:
time: 166 us
  waiting for transfers between devices  90.6 us (55%)
  Pallas kernels  57.2 us (34%)
  starting transfers between devices  16.7 us (10%)
    ppermute x8, waiting for transfers between devices, per_device(): in_flight[slot + 2] = lax.ppermute(passed, 'section', pairs)  62.1 us
    ppermute x9, waiting for transfers between devices, exchange(): return lax.ppermute(value, 'dp', pairs)  28.5 us
    pallas_call x9, Pallas kernels, backward(): pl.pallas_call(functools.partial(backward_body, slot, sections, arriving...  13.7 us
    pallas_call x1, Pallas kernels, recompute_first(): pl.pallas_call(functools.partial(first_body, sections), out_shape=(kept_o...  11.7 us
    pallas_call x3, Pallas kernels, recompute(): pl.pallas_call(functools.partial(recompute_body, slot, sections), out_sha...  10.1 us
    pallas_call x3, Pallas kernels, weights_step(): pl.pallas_call(functools.partial(weights_body, index), out_shape=(*(kept_...  8.92 us
    ppermute x9, starting transfers between devices, exchange(): return lax.ppermute(value, 'dp', pairs)  8.51 us
    ppermute x8, starting transfers between devices, per_device(): in_flight[slot + 2] = lax.ppermute(passed, 'section', pairs)  8.24 us
  transfers between devices with their start and end apart: 17, of which 10 were waited for; matrix products, arithmetic and copies ran while one was open for 0% of the time, Pallas kernels for 21%

profile of v2, /device:TPU:0, one launch (start us, length us, event | category | flops | bytes accessed | tf_op | source)
XLA Modules:
  0.0 166.2 jit_solution(10428070800751897218)
XLA Ops:
  1.4 11.7 %recompute_first.1 = (bf16[1280,1920]{1,0:T(8,128)(2,1)S(1)}, bf16[640,1280]{1,0:T(8,128)(2,1)S(1)}, f32[1280,128]{1,0:T(8,128)S(1)}, f32[1,1280]{1,0:T(1,128)S(...) custom-call(s32[10]{0:T(128)S(1)} %pad_add_fusion.scalars, ...), custom_call_target="tpu_custom_call" | custom-call | tf_op jit(solution)/shard_map/recompute_first/pallas_call | solution.py:528
  14.4 4.5 %recompute.3 = (bf16[4,1920,256]{2,1,0:T(8,128)(2,1)S(1)}, bf16[32,256,80]{2,1,0:T(8,128)(2,1)S(1)}, bf16[32,256,256]{2,1,0:T(8,128)(2,1)S(1)}, bf16[4,1280,256]...) custom-call(s32[10]{0:T(128)S(1)} %pad_add_fusion.scalars, ...), custom_call_target="tpu_custom_call", output_to_operand_aliasing={{0}: (5, {}), {1}: (6, {}), {2}: (7, {}), {3}: (8, {}), {4}... | custom-call | tf_op jit(solution)/shard_map/recompute/pallas_call | solution.py:548
  20.2 4.9 %recompute.4 = (bf16[4,1920,256]{2,1,0:T(8,128)(2,1)S(1)}, bf16[32,256,80]{2,1,0:T(8,128)(2,1)S(1)}, bf16[32,256,256]{2,1,0:T(8,128)(2,1)S(1)}, bf16[4,1280,256]...) custom-call(s32[10]{0:T(128)S(1)} %pad_add_fusion.scalars, ...), custom_call_target="tpu_custom_call", output_to_operand_aliasing={{0}: (5, {}), {1}: (6, {}), {2}: (7, {}), {3}: (8, {}), {4}... | custom-call | tf_op jit(solution)/shard_map/recompute/pallas_call | solution.py:548
  28.9 1.3 collective-permute-start.5
  30.8 1.3 collective-permute-start.4
  32.1 38.8 %collective-permute-done.5.refs_0_ = bf16[1280,256]{1,0:T(8,128)(2,1)S(1)} collective-permute-done((bf16[1280,256]{1,0:T(8,128)(2,1)S(1)}, bf16[1280,256]{1,0:T(8,128)(2,1)S(1)}, u32[]{:S(2)}, u32[]{:S(2)}) %collective-permute-start.5) | collective-permute-done | bytes 655392 | tf_op jit(solution)/shard_map/ppermute | solution.py:642
  70.9 3.4 %backward.15 = (bf16[1280,256]{1,0:T(8,128)(2,1)S(1)}, bf16[4,1920,256]{2,1,0:T(8,128)(2,1)S(1)}, bf16[4,1280,256]{2,1,0:T(8,128)(2,1)S(1)}) custom-call(s32[10]{0:T(128)S(1)} %pad_add_fusion.scalars, bf16[1280,256]{1,0:T(8,128)(2,1)S(1)} %collective-permute-done.5.refs_0_, ...), custom_call_target="tpu_custom_call", output_to_operand_aliasing={{1}: (10, {}), {2}: (11, {})} | custom-call | tf_op jit(solution)/shard_map/backward/pallas_call | solution.py:572
  74.3 1.6 collective-permute-start.7
  75.9 3.0 %weights.3 = (bf16[1280,1200]{1,0:T(8,128)(2,1)S(1)}, bf16[1280,720]{1,0:T(8,128)(2,1)S(1)}, bf16[1280,640]{1,0:T(8,128)(2,1)S(1)}) custom-call(bf16[4,1280,256]{2,1,0:T(8,128)(2,1)S(1)} %get-tuple-element.167.hidden.refs_6_.refs_5_, bf16[4,640,256]{2,1,0:T(8,128)(2,1)S(1)} %get-tuple-element.168.attn, ...), custom_call_target="tpu_custom_call" | custom-call | tf_op jit(solution)/shard_map/weights/pallas_call | solution.py:597
  78.9 8.5 %collective-permute-done.4.refs_0_ = bf16[1280,256]{1,0:T(8,128)(2,1)S(1)} collective-permute-done((bf16[1280,256]{1,0:T(8,128)(2,1)S(1)}, bf16[1280,256]{1,0:T(8,128)(2,1)S(1)}, u32[]{:S(2)}, u32[]{:S(2)}) %collective-permute-start.4) | collective-permute-done | bytes 655392 | tf_op jit(solution)/shard_map/ppermute | solution.py:642
  87.4 3.4 %backward.16 = (bf16[1280,256]{1,0:T(8,128)(2,1)S(1)}, bf16[4,1920,256]{2,1,0:T(8,128)(2,1)S(1)}, bf16[4,1280,256]{2,1,0:T(8,128)(2,1)S(1)}) custom-call(s32[10]{0:T(128)S(1)} %pad_add_fusion.scalars, bf16[1280,256]{1,0:T(8,128)(2,1)S(1)} %collective-permute-done.4.refs_0_, ...), custom_call_target="tpu_custom_call", output_to_operand_aliasing={{1}: (10, {}), {2}: (11, {})} | custom-call | tf_op jit(solution)/shard_map/backward/pallas_call | solution.py:572
  90.8 1.3 collective-permute-start.6
  92.1 3.0 %weights.4 = (bf16[1280,1200]{1,0:T(8,128)(2,1)S(1)}, bf16[1280,720]{1,0:T(8,128)(2,1)S(1)}, bf16[1280,640]{1,0:T(8,128)(2,1)S(1)}) custom-call(bf16[4,1280,256]{2,1,0:T(8,128)(2,1)S(1)} %get-tuple-element.167.hidden.refs_6_.refs_5_, bf16[4,640,256]{2,1,0:T(8,128)(2,1)S(1)} %get-tuple-element.168.attn, ...), custom_call_target="tpu_custom_call", output_to_operand_aliasing={{0}: (4, {}), {1}: (5, {}), {2}: (6, {})} | custom-call | tf_op jit(solution)/shard_map/weights/pallas_call | solution.py:597
  95.1 5.1 %collective-permute-done.7.refs_0_ = bf16[1280,256]{1,0:T(8,128)(2,1)S(1)} collective-permute-done((bf16[1280,256]{1,0:T(8,128)(2,1)S(1)}, bf16[1280,256]{1,0:T(8,128)(2,1)S(1)}, u32[]{:S(2)}, u32[]{:S(2)}) %collective-permute-start.7) | collective-permute-done | bytes 655392 | tf_op jit(solution)/shard_map/ppermute | solution.py:642
  100.2 3.4 %backward.17 = (bf16[4,1920,256]{2,1,0:T(8,128)(2,1)S(1)}, bf16[4,1280,256]{2,1,0:T(8,128)(2,1)S(1)}) custom-call(s32[10]{0:T(128)S(1)} %pad_add_fusion.scalars, bf16[1280,256]{1,0:T(8,128)(2,1)S(1)} %collective-permute-done.7.refs_0_, ...), custom_call_target="tpu_custom_call", output_to_operand_aliasing={{0}: (10, {}), {1}: (11, {})} | custom-call | tf_op jit(solution)/shard_map/backward/pallas_call | solution.py:572
  103.7 3.0 %weights.5 = (bf16[1280,1200]{1,0:T(8,128)(2,1)S(1)}, bf16[1280,720]{1,0:T(8,128)(2,1)S(1)}, bf16[1280,640]{1,0:T(8,128)(2,1)S(1)}) custom-call(bf16[4,1280,256]{2,1,0:T(8,128)(2,1)S(1)} %get-tuple-element.167.hidden.refs_6_.refs_5_, bf16[4,640,256]{2,1,0:T(8,128)(2,1)S(1)} %get-tuple-element.168.attn, ...), custom_call_target="tpu_custom_call", output_to_operand_aliasing={{0}: (4, {}), {1}: (5, {}), {2}: (6, {})} | custom-call | tf_op jit(solution)/shard_map/weights/pallas_call | solution.py:597
  106.7 9.6 %collective-permute-done.6.refs_0_ = bf16[1280,256]{1,0:T(8,128)(2,1)S(1)} collective-permute-done((bf16[1280,256]{1,0:T(8,128)(2,1)S(1)}, bf16[1280,256]{1,0:T(8,128)(2,1)S(1)}, u32[]{:S(2)}, u32[]{:S(2)}) %collective-permute-start.6) | collective-permute-done | bytes 655392 | tf_op jit(solution)/shard_map/ppermute | solution.py:642
  116.3 4.6 %tail_qkv.2 = (bf16[4,160,1200]{2,1,0:T(8,128)(2,1)S(1)}, bf16[4,160,1200]{2,1,0:T(8,128)(2,1)S(1)}, bf16[4,1280,256]{2,1,0:T(8,128)(2,1)S(1)}) custom-call(s32[10]{0:T(128)S(1)} %pad_add_fusion.scalars, bf16[1280,256]{1,0:T(8,128)(2,1)S(1)} %collective-permute-done.6.refs_0_, ...), custom_call_target="tpu_custom_call", output_to_operand_aliasing={{2}: (6, {})} | custom-call | tf_op jit(solution)/shard_map/tail_qkv/pallas_call | solution.py:659
  120.9 2.0 %tail_out.1 = (bf16[4,160,640]{2,1,0:T(8,128)(2,1)S(1)}, bf16[4,160,640]{2,1,0:T(8,128)(2,1)S(1)}) custom-call(s32[10]{0:T(128)S(1)} %pad_add_fusion.scalars, bf16[4,1280,256]{2,1,0:T(8,128)(2,1)S(1)} %get-tuple-element.178.masked.refs_4_, bf16[4,640,256]{2,1,0:T(8,128)(2,1)S(1)} %get-tuple-element.168.attn, bf16[1280,640]{1,0:T(8,128)(2,1)S(1)} %get-tuple-element.179.acc_out), custom_call_target="tpu_custom_call" | custom-call | tf_op jit(solution)/shard_map/tail_out/pallas_call | solution.py:675
  123.5 1.0 collective-permute-done.8.arrived
  124.8 0.8 collective-permute-done.9.arrived
  125.8 3.4 %tail_qkv.3 = (bf16[4,160,720]{2,1,0:T(8,128)(2,1)S(1)}, bf16[4,160,720]{2,1,0:T(8,128)(2,1)S(1)}) custom-call(s32[10]{0:T(128)S(1)} %pad_add_fusion.scalars, bf16[640,1280]{1,0:T(8,128)(2,1)S(1)} %get-tuple-element.106.refs_1_.refs_2_.refs_0_, bf16[4,1920,256]{2,1,0:T(8,128)(2,1)S(1)} %get-tuple-element.143.refs_4_.refs_2_.refs_1_, ...), custom_call_target="tpu_custom_call" | custom-call | tf_op jit(solution)/shard_map/tail_qkv/pallas_call | solution.py:659
  129.5 1.5 collective-permute-start.11
  131.0 1.5 collective-permute-start.10
  132.7 0.9 collective-permute-start.14
  133.7 9.6 %collective-permute-done.10.arrived = bf16[2,160,640]{2,1,0:T(8,128)(2,1)S(1)} collective-permute-done((bf16[2,160,640]{2,1,0:T(8,128)(2,1)S(1)}, bf16[2,160,640]{2,1,0:T(8,128)(2,1)S(1)}, u32[]{:S(2)}, u32[]{:S(2)}) %collective-permute-start.10) | collective-permute-done | bytes 409632 | tf_op jit(solution)/shard_map/ppermute | solution.py:613
  143.4 6.5 %collective-permute-done.11.arrived = bf16[2,160,1200]{2,1,0:T(8,128)(2,1)S(1)} collective-permute-done((bf16[2,160,1200]{2,1,0:T(8,128)(2,1)S(1)}, bf16[2,160,1200]{2,1,0:T(8,128)(2,1)S(1)}, u32[]{:S(2)}, u32[]{:S(2)}) %collective-permute-start.11) | collective-permute-done | bytes 768032 | tf_op jit(solution)/shard_map/ppermute | solution.py:613
  150.2 1.6 collective-permute-start.12
  151.8 1.7 %collective-permute-done.14.arrived = bf16[2,160,720]{2,1,0:T(8,128)(2,1)S(1)} collective-permute-done((bf16[2,160,720]{2,1,0:T(8,128)(2,1)S(1)}, bf16[2,160,720]{2,1,0:T(8,128)(2,1)S(1)}, u32[]{:S(2)}, u32[]{:S(2)}) %collective-permute-start.14) | collective-permute-done | bytes 460832 | tf_op jit(solution)/shard_map/ppermute | solution.py:613
  153.7 2.0 %collective-permute-start.16 = (bf16[1,160,640]{2,1,0:T(8,128)(2,1)S(1)}, bf16[1,160,640]{2,1,0:T(8,128)(2,1)S(1)}, u32[]{:S(2)}, u32[]{:S(2)}) collective-permute-start(bf16[1,160,640]{2,1,0:T(8,128)(2,1)S(1)} %get-tuple-element.205), channel_id=1, source_target_pairs={{0,2},{1,3},{2,0},{3,1},{4,6},{5,7},{6,4},{7,5},{8,10},{9,11},{10,... | collective-permute-start | bytes 614408 | tf_op jit(solution)/shard_map/ppermute | solution.py:613
  155.7 8.8 %collective-permute-done.16.refs_5_ = bf16[1,160,640]{2,1,0:T(8,128)(2,1)S(1)} collective-permute-done((bf16[1,160,640]{2,1,0:T(8,128)(2,1)S(1)}, bf16[1,160,640]{2,1,0:T(8,128)(2,1)S(1)}, u32[]{:S(2)}, u32[]{:S(2)}) %collective-permute-start.16) | collective-permute-done | bytes 204832 | tf_op jit(solution)/shard_map/ppermute | solution.py:613
  164.6 1.6 finish.1
  (29 shorter events, 9.8 us)
Async XLA Ops:
  13.6 11.5 %collective-permute-start.1 = (bf16[1280,256]{1,0:T(8,128)(2,1)S(1)}, bf16[1280,256]{1,0:T(8,128)(2,1)S(1)}, u32[]{:S(2)}, u32[]{:S(2)}) collective-permute-start(bf16[1280,256]{1,0:T(8,128)(2,1)S(1)} %get-tuple-element.138), channel_id=1, source_target_pairs={{24,16},{25,17},{26,18},{27,19},{28,20},{29,21},{30,22},{31,23}} | collective-permute-start | bytes 1966088 | tf_op jit(solution)/shard_map/ppermute | solution.py:642
  19.5 7.5 %collective-permute-start = (bf16[1280,256]{1,0:T(8,128)(2,1)S(1)}, bf16[1280,256]{1,0:T(8,128)(2,1)S(1)}, u32[]{:S(2)}, u32[]{:S(2)}) collective-permute-start(bf16[1280,256]{1,0:T(8,128)(2,1)S(1)} %get-tuple-element.126), channel_id=1, source_target_pairs={{24,16},{25,17},{26,18},{27,19},{28,20},{29,21},{30,22},{31,23}} | collective-permute-start | bytes 1966088 | tf_op jit(solution)/shard_map/ppermute | solution.py:642
  25.7 2.6 %collective-permute-start.3 = (bf16[1280,256]{1,0:T(8,128)(2,1)S(1)}, bf16[1280,256]{1,0:T(8,128)(2,1)S(1)}, u32[]{:S(2)}, u32[]{:S(2)}) collective-permute-start(bf16[1280,256]{1,0:T(8,128)(2,1)S(1)} %get-tuple-element.151), channel_id=1, source_target_pairs={{16,8},{24,16},{17,9},{25,17},{18,10},{26,18},{19,11},{27,19},{20,... | collective-permute-start | bytes 1966088 | tf_op jit(solution)/shard_map/ppermute | solution.py:642
  27.6 2.6 %collective-permute-start.2 = (bf16[1280,256]{1,0:T(8,128)(2,1)S(1)}, bf16[1280,256]{1,0:T(8,128)(2,1)S(1)}, u32[]{:S(2)}, u32[]{:S(2)}) collective-permute-start(bf16[1280,256]{1,0:T(8,128)(2,1)S(1)} %get-tuple-element.150), channel_id=1, source_target_pairs={{16,8},{24,16},{17,9},{25,17},{18,10},{26,18},{19,11},{27,19},{20,... | collective-permute-start | bytes 1966088 | tf_op jit(solution)/shard_map/ppermute | solution.py:642
  28.9 42.0 %collective-permute-start.5 = (bf16[1280,256]{1,0:T(8,128)(2,1)S(1)}, bf16[1280,256]{1,0:T(8,128)(2,1)S(1)}, u32[]{:S(2)}, u32[]{:S(2)}) collective-permute-start(bf16[1280,256]{1,0:T(8,128)(2,1)S(1)} %get-tuple-element.157), channel_id=1, source_target_pairs={{8,0},{16,8},{9,1},{17,9},{10,2},{18,10},{11,3},{19,11},{12,4},{20... | collective-permute-start | bytes 1966088 | tf_op jit(solution)/shard_map/ppermute | solution.py:642
  30.8 56.6 %collective-permute-start.4 = (bf16[1280,256]{1,0:T(8,128)(2,1)S(1)}, bf16[1280,256]{1,0:T(8,128)(2,1)S(1)}, u32[]{:S(2)}, u32[]{:S(2)}) collective-permute-start(bf16[1280,256]{1,0:T(8,128)(2,1)S(1)} %get-tuple-element.156), channel_id=1, source_target_pairs={{8,0},{16,8},{9,1},{17,9},{10,2},{18,10},{11,3},{19,11},{12,4},{20... | collective-permute-start | bytes 1966088 | tf_op jit(solution)/shard_map/ppermute | solution.py:642
  74.3 25.9 %collective-permute-start.7 = (bf16[1280,256]{1,0:T(8,128)(2,1)S(1)}, bf16[1280,256]{1,0:T(8,128)(2,1)S(1)}, u32[]{:S(2)}, u32[]{:S(2)}) collective-permute-start(bf16[1280,256]{1,0:T(8,128)(2,1)S(1)} %get-tuple-element.163), channel_id=1, source_target_pairs={{8,0},{9,1},{10,2},{11,3},{12,4},{13,5},{14,6},{15,7}} | collective-permute-start | bytes 1966088 | tf_op jit(solution)/shard_map/ppermute | solution.py:642
  90.8 25.5 %collective-permute-start.6 = (bf16[1280,256]{1,0:T(8,128)(2,1)S(1)}, bf16[1280,256]{1,0:T(8,128)(2,1)S(1)}, u32[]{:S(2)}, u32[]{:S(2)}) collective-permute-start(bf16[1280,256]{1,0:T(8,128)(2,1)S(1)} %get-tuple-element.162), channel_id=1, source_target_pairs={{8,0},{9,1},{10,2},{11,3},{12,4},{13,5},{14,6},{15,7}} | collective-permute-start | bytes 1966088 | tf_op jit(solution)/shard_map/ppermute | solution.py:642
  120.9 3.6 %collective-permute-start.8 = (bf16[4,160,1200]{2,1,0:T(8,128)(2,1)S(1)}, bf16[4,160,1200]{2,1,0:T(8,128)(2,1)S(1)}, u32[]{:S(2)}, u32[]{:S(2)}) collective-permute-start(bf16[4,160,1200]{2,1,0:T(8,128)(2,1)S(1)} %get-tuple-element.183), channel_id=1, source_target_pairs={{0,1},{1,0},{2,3},{3,2},{4,5},{5,4},{6,7},{7,6},{8,9},{9,8},{10,11... | collective-permute-start | bytes 4608008 | tf_op jit(solution)/shard_map/ppermute | solution.py:613
  122.9 2.7 %collective-permute-start.9 = (bf16[4,160,640]{2,1,0:T(8,128)(2,1)S(1)}, bf16[4,160,640]{2,1,0:T(8,128)(2,1)S(1)}, u32[]{:S(2)}, u32[]{:S(2)}) collective-permute-start(bf16[4,160,640]{2,1,0:T(8,128)(2,1)S(1)} %get-tuple-element.187), channel_id=1, source_target_pairs={{0,1},{1,0},{2,3},{3,2},{4,5},{5,4},{6,7},{7,6},{8,9},{9,8},{10,11... | collective-permute-start | bytes 2457608 | tf_op jit(solution)/shard_map/ppermute | solution.py:613
  129.2 3.3 %collective-permute-start.13 = (bf16[4,160,720]{2,1,0:T(8,128)(2,1)S(1)}, bf16[4,160,720]{2,1,0:T(8,128)(2,1)S(1)}, u32[]{:S(2)}, u32[]{:S(2)}) collective-permute-start(bf16[4,160,720]{2,1,0:T(8,128)(2,1)S(1)} %get-tuple-element.199), channel_id=1, source_target_pairs={{0,1},{1,0},{2,3},{3,2},{4,5},{5,4},{6,7},{7,6},{8,9},{9,8},{10,11... | collective-permute-start | bytes 2764808 | tf_op jit(solution)/shard_map/ppermute | solution.py:613
  129.5 20.5 %collective-permute-start.11 = (bf16[2,160,1200]{2,1,0:T(8,128)(2,1)S(1)}, bf16[2,160,1200]{2,1,0:T(8,128)(2,1)S(1)}, u32[]{:S(2)}, u32[]{:S(2)}) collective-permute-start(bf16[2,160,1200]{2,1,0:T(8,128)(2,1)S(1)} %get-tuple-element.193), channel_id=1, source_target_pairs={{0,2},{1,3},{2,0},{3,1},{4,6},{5,7},{6,4},{7,5},{8,10},{9,11},{10,... | collective-permute-start | bytes 2304008 | tf_op jit(solution)/shard_map/ppermute | solution.py:613
  131.0 12.3 %collective-permute-start.10 = (bf16[2,160,640]{2,1,0:T(8,128)(2,1)S(1)}, bf16[2,160,640]{2,1,0:T(8,128)(2,1)S(1)}, u32[]{:S(2)}, u32[]{:S(2)}) collective-permute-start(bf16[2,160,640]{2,1,0:T(8,128)(2,1)S(1)} %get-tuple-element.190), channel_id=1, source_target_pairs={{0,4},{1,5},{2,6},{3,7},{4,0},{5,1},{6,2},{7,3},{8,12},{9,13},{10,... | collective-permute-start | bytes 1228808 | tf_op jit(solution)/shard_map/ppermute | solution.py:613
  132.7 20.8 %collective-permute-start.14 = (bf16[2,160,720]{2,1,0:T(8,128)(2,1)S(1)}, bf16[2,160,720]{2,1,0:T(8,128)(2,1)S(1)}, u32[]{:S(2)}, u32[]{:S(2)}) collective-permute-start(bf16[2,160,720]{2,1,0:T(8,128)(2,1)S(1)} %get-tuple-element.201), channel_id=1, source_target_pairs={{0,4},{1,5},{2,6},{3,7},{4,0},{5,1},{6,2},{7,3},{8,12},{9,13},{10,... | collective-permute-start | bytes 1382408 | tf_op jit(solution)/shard_map/ppermute | solution.py:613
  150.2 14.3 %collective-permute-start.12 = (bf16[1,160,1200]{2,1,0:T(8,128)(2,1)S(1)}, bf16[1,160,1200]{2,1,0:T(8,128)(2,1)S(1)}, u32[]{:S(2)}, u32[]{:S(2)}) collective-permute-start(bf16[1,160,1200]{2,1,0:T(8,128)(2,1)S(1)} %get-tuple-element.195), channel_id=1, source_target_pairs={{0,4},{1,5},{2,6},{3,7},{4,0},{5,1},{6,2},{7,3},{8,12},{9,13},{10,... | collective-permute-start | bytes 1152008 | tf_op jit(solution)/shard_map/ppermute | solution.py:613
  153.6 10.9 %collective-permute-start.15 = (bf16[1,160,720]{2,1,0:T(8,128)(2,1)S(1)}, bf16[1,160,720]{2,1,0:T(8,128)(2,1)S(1)}, u32[]{:S(2)}, u32[]{:S(2)}) collective-permute-start(bf16[1,160,720]{2,1,0:T(8,128)(2,1)S(1)} %get-tuple-element.203), channel_id=1, source_target_pairs={{0,2},{1,3},{2,0},{3,1},{4,6},{5,7},{6,4},{7,5},{8,10},{9,11},{10,... | collective-permute-start | bytes 691208 | tf_op jit(solution)/shard_map/ppermute | solution.py:613
  153.7 10.8 %collective-permute-start.16 = (bf16[1,160,640]{2,1,0:T(8,128)(2,1)S(1)}, bf16[1,160,640]{2,1,0:T(8,128)(2,1)S(1)}, u32[]{:S(2)}, u32[]{:S(2)}) collective-permute-start(bf16[1,160,640]{2,1,0:T(8,128)(2,1)S(1)} %get-tuple-element.205), channel_id=1, source_target_pairs={{0,2},{1,3},{2,0},{3,1},{4,6},{5,7},{6,4},{7,5},{8,10},{9,11},{10,... | collective-permute-start | bytes 614408 | tf_op jit(solution)/shard_map/ppermute | solution.py:613
